TPU v7x, 32 devices: a whole 2x2x4 slice. The times are simulated.
32 devices in a mesh: dp: 4 (over z), row: 4 (over x, core), col: 2 (over y).
Axes of the slice: x: 2, y: 2, z: 4, core: 2. Of those that a mesh axis runs over, the one named last changes fastest.
Arguments:
- tokens: bfloat16 [512, 4096], P('dp', 'row'), may hold values from -6 to 6
- cotangent: bfloat16 [512, 4096], P('dp', 'row'), may hold values from -6 to 6
- weight_in: bfloat16 [4096, 15360], P('row', 'col'), may hold values from -0.09375 to 0.09375
- weight_out: bfloat16 [4096, 15360], P('row', 'col'), may hold values from -0.046875 to 0.046875
Outputs:
- outputs: bfloat16 [512, 4096], P(('dp', 'col'), 'row')
- token_gradient: bfloat16 [512, 4096], P(('dp', 'col'), 'row')
- weight_in_gradient: float32 [4096, 15360], P('row', ('col', 'dp'))
- weight_out_gradient: float32 [4096, 15360], P('row', ('col', 'dp'))
All inputs are finite; a program needn't handle non-finite values.
Results may differ from a plain program's by a relative error of at most 0.017.
Values may be sent and summed in bfloat16 or wider, within the bound.
A program may use at most 192 MiB of HBM per device.

v0:
```python
import jax
import jax.numpy as jnp
from jax import lax
from jax.sharding import PartitionSpec as P

root_half = 0.7071067811865476
inv_root_tau = 0.3989422804014327


def gelu_pair(hidden):
    normal_cdf = 0.5 * (1.0 + lax.erf(hidden * root_half))
    density = jnp.exp(-0.5 * hidden * hidden) * inv_root_tau
    return (hidden * normal_cdf, normal_cdf + hidden * density)


def slice_product(left, right):
    return jnp.dot(left, right, preferred_element_type=jnp.float32)


def slice_product_across(left, right):
    return lax.dot_general(
        left, right, (((1,), (1,)), ((), ())), preferred_element_type=jnp.float32
    )


def row_partial(left, right):
    return lax.psum_scatter(
        slice_product(left, right).astype(jnp.bfloat16), "row", scatter_dimension=0, tiled=True
    ).astype(jnp.float32)


def gather_rows(values):
    return lax.all_gather(values, "row", axis=0, tiled=True)


def column_partial(left, right):
    return lax.psum_scatter(
        slice_product_across(left, right).astype(jnp.bfloat16),
        "col",
        scatter_dimension=0,
        tiled=True,
    ).astype(jnp.float32)


def shards(tokens, cotangent, weight_in, weight_out):
    group_tokens = tokens.shape[0]
    factor = 1.0 / (group_tokens * lax.axis_size("dp"))
    hidden = row_partial(tokens, weight_in)
    active_val, slope_val = gelu_pair(hidden)
    active = gather_rows(active_val.astype(jnp.bfloat16))
    outputs = column_partial(active, weight_out).astype(jnp.bfloat16)
    hidden_grad = gather_rows((row_partial(cotangent, weight_out) * slope_val).astype(jnp.bfloat16))
    token_gradient = column_partial(hidden_grad, weight_in).astype(jnp.bfloat16)
    contract = (((0,), (0,)), ((), ()))
    term_in = (
        lax.dot_general(tokens, hidden_grad, contract, preferred_element_type=jnp.float32) * factor
    )
    term_out = (
        lax.dot_general(cotangent, active, contract, preferred_element_type=jnp.float32) * factor
    )
    weight_in_gradient, weight_out_gradient = (
        lax.psum_scatter(
            term_in.astype(jnp.bfloat16), "dp", scatter_dimension=1, tiled=True
        ).astype(jnp.float32),
        lax.psum_scatter(
            term_out.astype(jnp.bfloat16), "dp", scatter_dimension=1, tiled=True
        ).astype(jnp.float32),
    )
    return (outputs, token_gradient, weight_in_gradient, weight_out_gradient)


def solution(mesh):
    return jax.shard_map(
        shards,
        mesh=mesh,
        in_specs=(P("dp", "row"), P("dp", "row"), P("row", "col"), P("row", "col")),
        out_specs=(
            P(("dp", "col"), "row"),
            P(("dp", "col"), "row"),
            P("row", ("col", "dp")),
            P("row", ("col", "dp")),
        ),
        check_vma=False,
    )
```

profile of v0, /device:TPU:0, one launch (start us, length us, event | category | flops | bytes accessed | tf_op | source)
XLA Modules:
  0.0 700.4 jit_solution(717316045191180239)
XLA Ops:
  7.2 0.0 copy-start
  7.2 0.0 copy-start.3
  7.2 0.0 reduce-scatter.7.cloned.1.call-start
  7.2 0.9 copy-done
  8.1 9.0 %convolution_convert_fusion.1 = bf16[128,7680]{1,0:T(8,128)(2,1)} fusion(bf16[128,1024]{1,0:T(8,128)(2,1)S(1)} %copy-done, bf16[1024,7680]{1,0:T(8,128)(2,1)} %param.6), kind=kOutput, calls=%fused_computation.5 | convolution fusion | flops 2014248960 | bytes 17956864 | tf_op jit(solution)/shard_map/dot_general | solution.py:17
  17.1 0.0 reduce-scatter.7.cloned.1.call-update
  17.1 0.0 reduce-scatter.11.cloned.1.call-start
  17.2 0.0 copy-done.3
  17.2 9.0 %convolution_convert_fusion = bf16[128,7680]{1,0:T(8,128)(2,1)} fusion(bf16[128,1024]{1,0:T(8,128)(2,1)S(1)} %copy-done.3, bf16[1024,7680]{1,0:T(8,128)(2,1)} %param.7), kind=kOutput, calls=%fused_computation.4 | convolution fusion | flops 2014248960 | bytes 17956864 | tf_op jit(solution)/shard_map/dot_general | solution.py:17
  26.2 0.0 reduce-scatter.11.cloned.1.call-update
  26.2 0.0 all-gather.5.cloned.1.call-start
  26.2 24.2 %reduce-scatter.7.cloned.1.call-done = bf16[32,7680]{1,0:T(8,128)(2,1)} async-done(((bf16[128,7680]{1,0:T(8,128)(2,1)}), bf16[32,7680]{1,0:T(8,128)(2,1)}) %reduce-scatter.7.cloned.1.call-update) | async-done | bytes 491536 | tf_op jit(solution)/shard_map/reduce_scatter | solution.py:27
  50.4 33.6 %reduce-scatter.11.cloned.1.call-done = bf16[32,7680]{1,0:T(8,128)(2,1)} async-done(((bf16[128,7680]{1,0:T(8,128)(2,1)}), bf16[32,7680]{1,0:T(8,128)(2,1)}) %reduce-scatter.11.cloned.1.call-update) | async-done | bytes 491536 | tf_op jit(solution)/shard_map/reduce_scatter | solution.py:27
  84.0 2.6 fusion.10
  86.6 0.0 all-gather.5.cloned.1.call-update
  86.6 0.0 all-gather.3.cloned.1.call-start
  86.7 0.5 all-gather.3.cloned.1.call-update
  87.2 0.0 reduce-scatter.15.cloned.1.call-start
  87.3 21.4 %all-gather.5.cloned.1.call-done = bf16[128,7680]{1,0:T(8,128)(2,1)} async-done(((bf16[32,7680]{1,0:T(8,128)(2,1)}), bf16[128,7680]{1,0:T(8,128)(2,1)}) %all-gather.5.cloned.1.call-update) | async-done | bytes 1966096 | tf_op jit(solution)/shard_map/all_gather | solution.py:33
  108.6 9.6 %fusion = bf16[1024,7680]{0,1:T(8,128)(2,1)} fusion(bf16[128,7680]{1,0:T(8,128)(2,1)} %all-gather.5.cloned.1.call-done, bf16[128,1024]{1,0:T(8,128)(2,1)S(1)} %copy-done), kind=kOutput, calls=%fused_computation.2 | convolution fusion | flops 2028994560 | bytes 17956864 | tf_op jit(solution)/shard_map/dot_general | solution.py:56
  118.2 0.0 reduce-scatter.15.cloned.1.call-update
  118.2 0.0 reduce-scatter.17.cloned.1.call-start
  118.3 14.2 %all-gather.3.cloned.1.call-done = bf16[128,7680]{1,0:T(8,128)(2,1)} async-done(((bf16[32,7680]{1,0:T(8,128)(2,1)}), bf16[128,7680]{1,0:T(8,128)(2,1)}) %all-gather.3.cloned.1.call-update) | async-done | bytes 1966096 | tf_op jit(solution)/shard_map/all_gather | solution.py:33
  132.5 10.2 %fusion.1 = bf16[1024,7680]{0,1:T(8,128)(2,1)} fusion(bf16[128,7680]{1,0:T(8,128)(2,1)} %all-gather.3.cloned.1.call-done, bf16[128,1024]{1,0:T(8,128)(2,1)S(1)} %copy-done.3), kind=kOutput, calls=%fused_computation.3 | convolution fusion | flops 2028994560 | bytes 17956864 | tf_op jit(solution)/shard_map/dot_general | solution.py:59
  142.7 0.0 copy-start.2
  142.7 0.0 reduce-scatter.17.cloned.1.call-update
  142.7 0.0 reduce-scatter.9.cloned.1.call-start
  142.7 12.0 %convolution_convert_fusion.3 = bf16[128,1024]{1,0:T(8,128)(2,1)} fusion(bf16[128,7680]{1,0:T(8,128)(2,1)} %all-gather.3.cloned.1.call-done, bf16[1024,7680]{1,0:T(8,128)(2,1)} %param.7), kind=kOutput, calls=%fused_computation.12 | convolution fusion | flops 2013396992 | bytes 17956864 | tf_op jit(solution)/shard_map/dot_general | solution.py:21
  154.7 0.0 reduce-scatter.9.cloned.1.call-update
  154.8 0.2 reduce-scatter.13.cloned.1.call-start
  155.0 0.0 copy-done.2
  155.0 0.0 copy-start.1
  155.0 11.3 %convolution_convert_fusion.2 = bf16[128,1024]{1,0:T(8,128)(2,1)} fusion(bf16[128,7680]{1,0:T(8,128)(2,1)S(1)} %copy-done.2, bf16[1024,7680]{1,0:T(8,128)(2,1)} %param.6), kind=kOutput, calls=%fused_computation.11 | convolution fusion | flops 2013396992 | bytes 17956864 | tf_op jit(solution)/shard_map/dot_general | solution.py:21
  166.3 0.0 reduce-scatter.13.cloned.1.call-update
  166.3 231.0 %reduce-scatter.15.cloned.1.call-done = bf16[1024,1920]{0,1:T(8,128)(2,1)} async-done(((bf16[1024,7680]{0,1:T(8,128)(2,1)}), bf16[1024,1920]{0,1:T(8,128)(2,1)}) %reduce-scatter.15.cloned.1.call-update) | async-done | bytes 3932176 | tf_op jit(solution)/shard_map/reduce_scatter | solution.py:62
  397.4 6.6 copy.8
  403.9 259.4 %reduce-scatter.17.cloned.1.call-done = bf16[1024,1920]{0,1:T(8,128)(2,1)} async-done(((bf16[1024,7680]{0,1:T(8,128)(2,1)}), bf16[1024,1920]{0,1:T(8,128)(2,1)}) %reduce-scatter.17.cloned.1.call-update) | async-done | bytes 3932176 | tf_op jit(solution)/shard_map/reduce_scatter | solution.py:65
  663.3 6.6 copy.9
  669.9 9.1 %reduce-scatter.9.cloned.1.call-done = bf16[64,1024]{1,0:T(8,128)(2,1)} async-done(((bf16[128,1024]{1,0:T(8,128)(2,1)}), bf16[64,1024]{1,0:T(8,128)(2,1)}) %reduce-scatter.9.cloned.1.call-update) | async-done | bytes 131088 | tf_op jit(solution)/shard_map/reduce_scatter | solution.py:37
  678.9 14.6 %reduce-scatter.13.cloned.1.call-done = bf16[64,1024]{1,0:T(8,128)(2,1)} async-done(((bf16[128,1024]{1,0:T(8,128)(2,1)}), bf16[64,1024]{1,0:T(8,128)(2,1)}) %reduce-scatter.13.cloned.1.call-update) | async-done | bytes 131088 | tf_op jit(solution)/shard_map/reduce_scatter | solution.py:37
  693.5 0.0 copy-done.1
Async XLA Ops:
  7.2 1.0 copy-start
  7.2 10.0 %copy-start.3 = (bf16[128,1024]{1,0:T(8,128)(2,1)S(1)}, bf16[128,1024]{1,0:T(8,128)(2,1)}, u32[]{:S(2)}) copy-start(bf16[128,1024]{1,0:T(8,128)(2,1)} %param.5) | copy-start | bytes 786436
  7.2 43.2 %reduce-scatter.7.cloned.1.call-start = ((), (), s32[]{:S(2)}) async-start(), calls=%async_computation.6 | async-start | bytes 2457600 | tf_op jit(solution)/shard_map/reduce_scatter | solution.py:27
  17.1 66.9 %reduce-scatter.11.cloned.1.call-start = ((), (), s32[]{:S(2)}) async-start(), calls=%async_computation.9 | async-start | bytes 2457600 | tf_op jit(solution)/shard_map/reduce_scatter | solution.py:27
  26.2 82.4 %all-gather.5.cloned.1.call-start = ((), (), s32[]{:S(2)}) async-start(), calls=%async_computation.10 | async-start | bytes 2457600 | tf_op jit(solution)/shard_map/all_gather | solution.py:33
  86.6 45.8 %all-gather.3.cloned.1.call-start = ((), (), s32[]{:S(2)}) async-start(), calls=%async_computation.7 | async-start | bytes 2457600 | tf_op jit(solution)/shard_map/all_gather | solution.py:33
  87.2 310.1 %reduce-scatter.15.cloned.1.call-start = ((), (), s32[]{:S(2)}) async-start(), calls=%async_computation.12 | async-start | bytes 19660800 | tf_op jit(solution)/shard_map/reduce_scatter | solution.py:62
  118.2 545.1 %reduce-scatter.17.cloned.1.call-start = ((), (), s32[]{:S(2)}) async-start(), calls=%async_computation.13 | async-start | bytes 19660800 | tf_op jit(solution)/shard_map/reduce_scatter | solution.py:65
  142.7 12.3 %copy-start.2 = (bf16[128,7680]{1,0:T(8,128)(2,1)S(1)}, bf16[128,7680]{1,0:T(8,128)(2,1)}, u32[]{:S(2)}) copy-start(bf16[128,7680]{1,0:T(8,128)(2,1)} %all-gather.5.cloned.1.call-done) | copy-start | bytes 5898244
  142.7 536.2 %reduce-scatter.9.cloned.1.call-start = ((), (), s32[]{:S(2)}) async-start(), calls=%async_computation.8 | async-start | bytes 393216 | tf_op jit(solution)/shard_map/reduce_scatter | solution.py:37
  154.8 538.8 %reduce-scatter.13.cloned.1.call-start = ((), (), s32[]{:S(2)}) async-start(), calls=%async_computation.11 | async-start | bytes 393216 | tf_op jit(solution)/shard_map/reduce_scatter | solution.py:37
  155.0 538.5 %copy-start.1 = (bf16[128,1024]{1,0:T(8,128)(2,1)S(1)}, bf16[128,1024]{1,0:T(8,128)(2,1)}, u32[]{:S(2)}) copy-start(bf16[128,1024]{1,0:T(8,128)(2,1)} %param.4) | copy-start | bytes 786436
Sparse Core Ops, SparseCore 0:
  17.2 33.1 reduce-scatter.6
  53.5 30.3 reduce-scatter.10
  86.8 21.8 all-gather.4
  110.6 21.8 all-gather.2
  134.7 262.6 reduce-scatter.14
  399.6 263.6 reduce-scatter.16
  666.1 12.7 reduce-scatter.8
  681.7 11.7 reduce-scatter.12
where the time goes:
time: 701 us; the launch traced here: 700 us
  waiting for transfers between devices  608 us (87%)
  matrix products  61 us (9%)
  between operations  14.2 us (2%)
  local copies, waits for them, and re-layouts  14 us (2%)
    reduce_scatter x1, waiting for transfers between devices, shards(): lax.psum_scatter(term_out.astype(jnp.bfloat16), 'dp', scatter_dimension=1...  259 us
    reduce_scatter x1, waiting for transfers between devices, shards(): lax.psum_scatter(term_in.astype(jnp.bfloat16), 'dp', scatter_dimension=1,...  231 us
    reduce_scatter x2, waiting for transfers between devices, row_partial(): lax.psum_scatter(slice_product(left, right).astype(jnp.bfloat16), 'row',...  57.7 us
    all_gather x2, waiting for transfers between devices, gather_rows(): return lax.all_gather(values, 'row', axis=0, tiled=True)  35.6 us
    reduce_scatter x2, waiting for transfers between devices, column_partial(): lax.psum_scatter(slice_product_across(left, right).astype(jnp.bfloat16),...  23.6 us
    dot_general x2, matrix products, slice_product_across(): lax.dot_general(left, right, (((1,), (1,)), ((), ())), preferred_element_...  23.3 us
    dot_general x2, matrix products, slice_product(): return jnp.dot(left, right, preferred_element_type=jnp.float32)  18 us
    unnamed x10, local copies, waits for them, and re-layouts  14 us
  transfers between devices with their start and end apart: 8, of which 8 were waited for; matrix products, arithmetic and copies ran while one was open for 9% of the time, Pallas kernels for 0%

commit v1 on v0

v1 whole, which is shorter than its diff:
```python
import jax
import jax.numpy as jnp
from jax import lax
from jax.experimental import pallas as pl
from jax.experimental.pallas import tpu as pltpu
from jax.sharding import PartitionSpec as P

root_half = 0.7071067811865476
inv_root_tau = 0.3989422804014327
F32 = jnp.float32
BF16 = jnp.bfloat16


def gelu_pair(hidden):
    normal_cdf = 0.5 * (1.0 + lax.erf(hidden * root_half))
    density = jnp.exp(-0.5 * hidden * hidden) * inv_root_tau
    return (hidden * normal_cdf, normal_cdf + hidden * density)


def dot(left, right):
    return jnp.dot(left, right, preferred_element_type=F32)


def dot_across(left, right):
    return lax.dot_general(left, right, (((1,), (1,)), ((), ())), preferred_element_type=F32)


def swap(values, axis, bit):
    n = lax.axis_size(axis)
    return lax.ppermute(values, axis, [(i, i ^ bit) for i in range(n)])


def take_half(values, which):
    half = values.shape[0] // 2
    return lax.dynamic_slice_in_dim(values, which * half, half, 0)


def after(values, earlier):
    return lax.optimization_barrier((values, earlier[:8, :128]))[0]


def shift(values, by):
    n = lax.axis_size("dp")
    return lax.ppermute(values, "dp", [(i, (i + by) % n) for i in range(n)])


def gather_tokens(values):
    groups, cols = lax.axis_size("dp"), lax.axis_size("col")
    kept = values.shape[0] // cols
    if cols == 2:
        side = lax.axis_index("col")
        first = lax.dynamic_slice_in_dim(values, side * kept, kept, 0)
        second = lax.dynamic_slice_in_dim(values, (1 - side) * kept, kept, 0)
        rows = [first, second]
        moved = [shift(first, by) for by in range(1, groups)]
        for part in moved:
            rows += [part, swap(part, "col", 1)]
        return jnp.concatenate(rows)
    gathered = lax.all_gather(values, "dp", axis=0, tiled=False)
    order = (lax.axis_index("dp") - jnp.arange(groups)) % groups
    return gathered[order].reshape(-1, values.shape[1])


def core_sum(mine, others, weights):
    given = swap(dot(others, weights).astype(BF16), "row", 1)
    return (dot(mine, weights) + given.astype(F32)).astype(BF16)


def row_total(part):
    total, bit = part, 2
    while bit < lax.axis_size("row"):
        total = total.astype(BF16)
        total = total.astype(F32) + swap(total, "row", bit).astype(F32)
        bit *= 2
    return total


def column_sum(rows, right):
    groups, cols = lax.axis_size("dp") // 2, lax.axis_size("col")
    product = dot_across(rows, right).astype(BF16)
    kept = rows.shape[0] // (groups * cols)
    blocks = product.reshape(groups, cols, kept, -1)
    if cols == 2:
        given = swap(blocks[:, 1].reshape(groups * kept, -1), "col", 1)
        total = blocks[:, 0].reshape(groups * kept, -1).astype(F32) + given.astype(F32)
        return total.astype(BF16)
    part = lax.psum_scatter(blocks, "col", scatter_dimension=1, tiled=True)
    return part.reshape(groups * kept, -1)


def group_sum(mine, others, side):
    groups = lax.axis_size("dp")
    ordered = jnp.where(
        side == 0, jnp.concatenate([mine, others]), jnp.concatenate([others, mine])
    ).reshape(groups, -1, mine.shape[1])
    total = ordered[0].astype(F32)
    for received in [shift(ordered[by], -by) for by in range(1, groups)]:
        total = total + received.astype(F32)
    return total.astype(BF16)


def gradient_kernel(factor, left_a, left_b, right_a, right_b, out):
    out[...] = (dot(left_a[...], right_a[...]) + dot(left_b[...], right_b[...])) * factor


def weight_gradient(left_a, left_b, right_a, right_b, factor):
    (feats, half), units = left_a.shape, right_a.shape[1]
    wide = next((w for w in (640, 512, 384, 256, 128) if units % w == 0), units)
    left = pl.BlockSpec((feats, half), lambda i: (0, 0))
    right = pl.BlockSpec((half, wide), lambda i: (0, i))
    return pl.pallas_call(
        lambda *refs: gradient_kernel(factor, *refs),
        out_shape=jax.ShapeDtypeStruct((feats, units), F32),
        grid=(units // wide,),
        in_specs=[left, left, right, right],
        out_specs=pl.BlockSpec((feats, wide), lambda i: (0, i)),
        cost_estimate=pl.CostEstimate(
            flops=4 * feats * half * units,
            bytes_accessed=4 * feats * units + 4 * half * (feats + units),
            transcendentals=0,
        ),
        compiler_params=pltpu.CompilerParams(vmem_limit_bytes=24 * 2**20),
    )(left_a, left_b, right_a, right_b)


def shards(tokens, cotangent, weight_in, weight_out):
    groups = lax.axis_size("dp")
    factor = 1.0 / (tokens.shape[0] * groups)
    units = weight_in.shape[1] // groups
    start = lax.axis_index("dp") * units
    up = lax.dynamic_slice_in_dim(weight_in, start, units, 1)
    down = lax.dynamic_slice_in_dim(weight_out, start, units, 1)
    side = lax.axis_index("row") % 2

    tokens = gather_tokens(tokens)
    cotangent = gather_tokens(cotangent)
    token_mine, token_others = take_half(tokens, side), take_half(tokens, 1 - side)
    hidden_part = core_sum(token_mine, token_others, up)
    hidden = row_total(hidden_part)

    cotangent = after(cotangent, hidden_part)
    cot_mine, cot_others = take_half(cotangent, side), take_half(cotangent, 1 - side)
    grad_part = core_sum(cot_mine, cot_others, down)
    grad = row_total(grad_part)

    active_val, slope_val = gelu_pair(hidden)
    active = active_val.astype(BF16)
    active_other = swap(active, "row", 1)
    output_mine = column_sum(active, down)
    output_others = column_sum(active_other, down)
    outputs = group_sum(output_mine, output_others, side)
    weight_out_gradient = weight_gradient(cot_mine.T, cot_others.T, active, active_other, factor)

    hidden_grad = (grad * slope_val).astype(BF16)
    hidden_grad_other = swap(hidden_grad, "row", 1)
    token_grad_mine = column_sum(hidden_grad, up)
    token_grad_others = column_sum(hidden_grad_other, up)
    token_gradient = group_sum(token_grad_mine, token_grad_others, side)
    weight_in_gradient = weight_gradient(
        token_mine.T, token_others.T, hidden_grad, hidden_grad_other, factor
    )
    return (outputs, token_gradient, weight_in_gradient, weight_out_gradient)


def solution(mesh):
    return jax.shard_map(
        shards,
        mesh=mesh,
        in_specs=(P("dp", "row"), P("dp", "row"), P("row", "col"), P("row", "col")),
        out_specs=(
            P(("dp", "col"), "row"),
            P(("dp", "col"), "row"),
            P("row", ("col", "dp")),
            P("row", ("col", "dp")),
        ),
        check_vma=False,
    )
```

time: 701 us -> 190 us (0.27)
  waiting for transfers between devices: 608 us -> 107 us
  matrix products: 61 us -> 30.6 us
  starting transfers between devices: 0.51 us -> 28.8 us
  between operations: 14.2 us -> 0.91 us
  Pallas kernels: 0 us -> 10.2 us
    reduce_scatter x6 -> x0, waiting for transfers between devices: 572 us -> none  [the longest x1 259 us: shards(): lax.psum_scatter(term_out.astype(jnp.bfloat16), 'dp', scatter_dimension=1...]
    ppermute x0 -> x28, waiting for transfers between devices: none -> 107 us  [the longest x16 64 us: swap(): return lax.ppermute(values, axis, [(i, i ^ bit) for i in range(n)])]
    all_gather x2 -> x0, waiting for transfers between devices: 35.6 us -> none  [gather_rows(): return lax.all_gather(values, 'row', axis=0, tiled=True)]
    dot_general x6 -> x8, matrix products: 61 us -> 30.6 us  [the longest x4 17 us: dot(): return jnp.dot(left, right, preferred_element_type=F32)]
    ppermute x0 -> x28, starting transfers between devices: none -> 28.8 us  [the longest x12 15.2 us: shift(): return lax.ppermute(values, 'dp', [(i, (i + by) % n) for i in range(n)])]
    unnamed x10 -> x4, local copies, waits for them, and re-layouts: 14 us -> 0.67 us
    pallas_call x0 -> x2, Pallas kernels: none -> 10.2 us  [weight_gradient(): pl.pallas_call(lambda *refs: gradient_kernel(factor, *refs), out_shape=ja...]
  transfers between devices with their start and end apart: 8 -> 28, of which waited for: 8 -> 16; matrix products, arithmetic and copies ran while one was open for 9% -> 18% of each run, Pallas kernels for 0% -> 5%
where the time goes in v1:
time: 190 us
  waiting for transfers between devices  107 us (56%)
  matrix products  30.6 us (16%)
  starting transfers between devices  28.8 us (15%)
  Pallas kernels  10.2 us (5%)
  local copies, waits for them, and re-layouts  7.02 us (4%)
  other arithmetic  4.69 us (2%)
    ppermute x16, waiting for transfers between devices, swap(): return lax.ppermute(values, axis, [(i, i ^ bit) for i in range(n)])  64 us
    ppermute x12, waiting for transfers between devices, shift(): return lax.ppermute(values, 'dp', [(i, (i + by) % n) for i in range(n)])  43.3 us
    dot_general x4, matrix products, dot(): return jnp.dot(left, right, preferred_element_type=F32)  17 us
    ppermute x12, starting transfers between devices, shift(): return lax.ppermute(values, 'dp', [(i, (i + by) % n) for i in range(n)])  15.2 us
    ppermute x16, starting transfers between devices, swap(): return lax.ppermute(values, axis, [(i, i ^ bit) for i in range(n)])  13.6 us
    dot_general x4, matrix products, dot_across(): lax.dot_general(left, right, (((1,), (1,)), ((), ())), preferred_element_...  13.6 us
    pallas_call x2, Pallas kernels, weight_gradient(): pl.pallas_call(lambda *refs: gradient_kernel(factor, *refs), out_shape=ja...  10.2 us
    concatenate x2, local copies, waits for them, and re-layouts, gather_tokens(): return jnp.concatenate(rows)  4.88 us
  transfers between devices with their start and end apart: 28, of which 16 were waited for; matrix products, arithmetic and copies ran while one was open for 18% of the time, Pallas kernels for 5%

profile of v1, /device:TPU:0, one launch (start us, length us, event | category | flops | bytes accessed | tf_op | source)
XLA Modules:
  0.0 189.5 jit_solution(10988319403465572512)
XLA Ops:
  0.6 1.1 constant_dynamic-slice_fusion
  1.8 0.2 copy.12
  1.9 5.1 %collective-permute-start.4 = (bf16[64,1024]{0,1:T(8,128)(2,1)S(1)}, bf16[64,1024]{0,1:T(8,128)(2,1)S(1)}, u32[]{:S(2)}, u32[]{:S(2)}) collective-permute-start(bf16[64,1024]{0,1:T(8,128)(2,1)S(1)} %copy.12), channel_id=1, source_target_pairs={{0,24},{8,0},{16,8},{24,16},{1,25},{9,1},{17,9},{25,17},{2,26},{10... | collective-permute-start | bytes 393224 | tf_op jit(solution)/shard_map/ppermute | solution.py:44
  7.1 1.0 collective-permute-start
  8.1 5.7 %collective-permute-done.4 = bf16[64,1024]{0,1:T(8,128)(2,1)S(1)} collective-permute-done((bf16[64,1024]{0,1:T(8,128)(2,1)S(1)}, bf16[64,1024]{0,1:T(8,128)(2,1)S(1)}, u32[]{:S(2)}, u32[]{:S(2)}) %collective-permute-start.4) | collective-permute-done | bytes 131104 | tf_op jit(solution)/shard_map/ppermute | solution.py:44
  13.8 1.5 collective-permute-start.5
  15.3 14.1 %collective-permute-done.2 = bf16[64,1024]{0,1:T(8,128)(2,1)S(1)} collective-permute-done((bf16[64,1024]{0,1:T(8,128)(2,1)S(1)}, bf16[64,1024]{0,1:T(8,128)(2,1)S(1)}, u32[]{:S(2)}, u32[]{:S(2)}) %collective-permute-start.2) | collective-permute-done | bytes 131104 | tf_op jit(solution)/shard_map/ppermute | solution.py:44
  29.4 1.5 collective-permute-start.3
  30.9 0.5 collective-permute-start.1
  31.4 0.2 copy.14
  31.7 2.4 %collective-permute-start.16 = (bf16[64,1024]{0,1:T(8,128)(2,1)S(1)}, bf16[64,1024]{0,1:T(8,128)(2,1)S(1)}, u32[]{:S(2)}, u32[]{:S(2)}) collective-permute-start(bf16[64,1024]{0,1:T(8,128)(2,1)S(1)} %copy.14), channel_id=1, source_target_pairs={{0,16},{8,24},{16,0},{24,8},{1,17},{9,25},{17,1},{25,9},{2,18},{10... | collective-permute-start | bytes 393224 | tf_op jit(solution)/shard_map/ppermute | solution.py:44
  34.0 0.2 copy.13
  34.2 2.0 %collective-permute-start.14 = (bf16[64,1024]{0,1:T(8,128)(2,1)S(1)}, bf16[64,1024]{0,1:T(8,128)(2,1)}, u32[]{:S(2)}, u32[]{:S(2)}) collective-permute-start(bf16[64,1024]{0,1:T(8,128)(2,1)S(1)} %copy.14), channel_id=1, source_target_pairs={{0,8},{8,16},{16,24},{24,0},{1,9},{9,17},{17,25},{25,1},{2,10},{10... | collective-permute-start | bytes 393224 | tf_op jit(solution)/shard_map/ppermute | solution.py:44
  36.2 2.5 %collective-permute-done.3 = bf16[64,1024]{0,1:T(8,128)(2,1)} collective-permute-done((bf16[64,1024]{0,1:T(8,128)(2,1)S(1)}, bf16[64,1024]{0,1:T(8,128)(2,1)}, u32[]{:S(2)}, u32[]{:S(2)}) %collective-permute-start.3) | collective-permute-done | bytes 131104 | tf_op jit(solution)/shard_map/ppermute | solution.py:30
  38.7 3.6 %collective-permute-done.1 = bf16[64,1024]{0,1:T(8,128)(2,1)} collective-permute-done((bf16[64,1024]{0,1:T(8,128)(2,1)S(1)}, bf16[64,1024]{0,1:T(8,128)(2,1)}, u32[]{:S(2)}, u32[]{:S(2)}) %collective-permute-start.1) | collective-permute-done | bytes 131104 | tf_op jit(solution)/shard_map/ppermute | solution.py:30
  42.3 2.4 %concatenate.18 = bf16[512,1024]{0,1:T(8,128)(2,1)S(1)} concatenate(bf16[64,1024]{0,1:T(8,128)(2,1)S(1)} %copy.12, bf16[64,1024]{0,1:T(8,128)(2,1)S(1)} %copy.13, bf16[64,1024]{0,1:T(8,128)(2,1)S(1)} %collective-permute-done, bf16[64,1024]{0,1:T(8,128)(2,1)} %collective-permute-done.1, bf16[64,1024]{0,1:T(8,128)(2,1)S(1)} %collective-permute-done.2, ...), dimensions={0} | concatenate | bytes 2097152 | tf_op jit(solution)/shard_map/concatenate | solution.py:58
  44.8 4.4 %convolution_convert_fusion.1 = bf16[256,1920]{1,0:T(8,128)(2,1)} fusion(bf16[1024,7680]{1,0:T(8,128)(2,1)} %param.6, s32[]{:T(128)S(6)} %select_n.44, bf16[512,1024]{0,1:T(8,128)(2,1)S(1)} %concatenate.18, s32[]{:T(128)S(6)} %select_n.45), kind=kOutput, calls=%fused_computation.4 | convolution fusion | flops 1007124480 | bytes 5439496 | tf_op jit(solution)/shard_map/dot_general | solution.py:21
  49.1 1.5 collective-permute-start.19
  50.6 5.6 %collective-permute-done.16 = bf16[64,1024]{0,1:T(8,128)(2,1)S(1)} collective-permute-done((bf16[64,1024]{0,1:T(8,128)(2,1)S(1)}, bf16[64,1024]{0,1:T(8,128)(2,1)S(1)}, u32[]{:S(2)}, u32[]{:S(2)}) %collective-permute-start.16) | collective-permute-done | bytes 131104 | tf_op jit(solution)/shard_map/ppermute | solution.py:44
  56.3 0.5 collective-permute-start.17
  56.8 1.5 collective-permute-start.15
  58.3 0.2 copy.15
  58.5 7.1 %collective-permute-done.17 = bf16[64,1024]{0,1:T(8,128)(2,1)} collective-permute-done((bf16[64,1024]{0,1:T(8,128)(2,1)S(1)}, bf16[64,1024]{0,1:T(8,128)(2,1)}, u32[]{:S(2)}, u32[]{:S(2)}) %collective-permute-start.17) | collective-permute-done | bytes 131104 | tf_op jit(solution)/shard_map/ppermute | solution.py:30
  65.6 3.6 %collective-permute-done.15 = bf16[64,1024]{0,1:T(8,128)(2,1)} collective-permute-done((bf16[64,1024]{0,1:T(8,128)(2,1)}, bf16[64,1024]{0,1:T(8,128)(2,1)}, u32[]{:S(2)}, u32[]{:S(2)}) %collective-permute-start.15) | collective-permute-done | bytes 131104 | tf_op jit(solution)/shard_map/ppermute | solution.py:30
  69.2 2.4 %concatenate.21 = bf16[512,1024]{0,1:T(8,128)(2,1)S(1)} concatenate(bf16[64,1024]{0,1:T(8,128)(2,1)S(1)} %copy.14, bf16[64,1024]{0,1:T(8,128)(2,1)S(1)} %copy.15, bf16[64,1024]{0,1:T(8,128)(2,1)} %collective-permute-done.14, bf16[64,1024]{0,1:T(8,128)(2,1)} %collective-permute-done.15, bf16[64,1024]{0,1:T(8,128)(2,1)S(1)} %collective-permute-done.16, ...), dimensions={0} | concatenate | bytes 2097152 | tf_op jit(solution)/shard_map/concatenate | solution.py:58
  71.6 4.4 %convolution_convert_fusion = bf16[256,1920]{1,0:T(8,128)(2,1)} fusion(bf16[1024,7680]{1,0:T(8,128)(2,1)} %param.7, s32[]{:T(128)S(6)} %select_n.44, bf16[512,1024]{0,1:T(8,128)(2,1)S(1)} %concatenate.21, s32[]{:T(128)S(6)} %select_n.45), kind=kOutput, calls=%fused_computation.3 | convolution fusion | flops 1007124480 | bytes 5439496 | tf_op jit(solution)/shard_map/dot_general | solution.py:21
  76.0 3.7 %fusion = bf16[256,1920]{1,0:T(8,128)(2,1)S(1)} fusion(bf16[1024,7680]{1,0:T(8,128)(2,1)} %param.6, s32[]{:T(128)S(6)} %select_n.44, bf16[256,1920]{1,0:T(8,128)(2,1)} %collective-permute-done.6, bf16[512,1024]{0,1:T(8,128)(2,1)S(1)} %concatenate.18, s32[]{:T(128)S(6)} %select_n.43), kind=kOutput, calls=%fused_computation.5 | convolution fusion | flops 1008107520 | bytes 6422536 | tf_op jit(solution)/shard_map/dot_general | solution.py:21
  79.7 1.6 collective-permute-start.7
  81.2 4.6 %fusion.1 = bf16[256,1920]{1,0:T(8,128)(2,1)} fusion(bf16[1024,7680]{1,0:T(8,128)(2,1)} %param.7, s32[]{:T(128)S(6)} %select_n.44, bf16[256,1920]{1,0:T(8,128)(2,1)} %collective-permute-done.20, bf16[512,1024]{0,1:T(8,128)(2,1)S(1)} %concatenate.21, s32[]{:T(128)S(6)} %select_n.43), kind=kOutput, calls=%fused_computation.6 | convolution fusion | flops 1008107520 | bytes 6422536 | tf_op jit(solution)/shard_map/dot_general | solution.py:21
  85.8 0.5 collective-permute-start.21
  86.5 18.0 %collective-permute-done.7 = bf16[256,1920]{1,0:T(8,128)(2,1)} collective-permute-done((bf16[256,1920]{1,0:T(8,128)(2,1)S(1)}, bf16[256,1920]{1,0:T(8,128)(2,1)}, u32[]{:S(2)}, u32[]{:S(2)}) %collective-permute-start.7) | collective-permute-done | bytes 983072 | tf_op jit(solution)/shard_map/ppermute | solution.py:30
  104.5 20.6 %collective-permute-done.21 = bf16[256,1920]{1,0:T(8,128)(2,1)} collective-permute-done((bf16[256,1920]{1,0:T(8,128)(2,1)}, bf16[256,1920]{1,0:T(8,128)(2,1)}, u32[]{:S(2)}, u32[]{:S(2)}) %collective-permute-start.21) | collective-permute-done | bytes 983072 | tf_op jit(solution)/shard_map/ppermute | solution.py:30
  125.1 2.6 %fusion.19 = (bf16[256,1920]{1,0:T(8,128)(2,1)S(1)}, bf16[256,1920]{1,0:T(8,128)(2,1)S(1)}) fusion(bf16[256,1920]{1,0:T(8,128)(2,1)} %collective-permute-done.21, bf16[256,1920]{1,0:T(8,128)(2,1)} %fusion.1, bf16[256,1920]{1,0:T(8,128)(2,1)} %collective-permute-done.7, bf16[256,1920]{1,0:T(8,128)(2,1)S(1)} %fusion), kind=kLoop, calls=%fused_computation.24 | loop fusion | flops 8847360 | bytes 5898240 | tf_op jit(solution)/shard_map/convert_element_type | solution.py:154
  127.8 3.4 %fusion.20 = bf16[256,1024]{1,0:T(8,128)(2,1)S(1)} fusion(bf16[256,1920]{1,0:T(8,128)(2,1)S(1)} %get-tuple-element.4.refs_2_, bf16[1024,7680]{1,0:T(8,128)(2,1)} %param.6, s32[]{:T(128)S(6)} %select_n.44), kind=kOutput, calls=%fused_computation.28 | convolution fusion | flops 1006895104 | bytes 5439492 | tf_op jit(solution)/shard_map/dot_general | solution.py:25
  131.2 0.1 collective-permute-start.23
  131.3 1.6 collective-permute-start.22
  132.9 3.4 %fusion.26 = bf16[256,1024]{1,0:T(8,128)(2,1)S(1)} fusion(bf16[256,1920]{1,0:T(8,128)(2,1)S(1)} %get-tuple-element.5.refs_2_, bf16[1024,7680]{1,0:T(8,128)(2,1)} %param.7, s32[]{:T(128)S(6)} %select_n.44), kind=kOutput, calls=%fused_computation.30 | convolution fusion | flops 1006895104 | bytes 5439492 | tf_op jit(solution)/shard_map/dot_general | solution.py:25
  136.3 0.6 collective-permute-start.8
  136.9 0.1 collective-permute-start.9
  137.0 3.5 %collective-permute-done.22 = bf16[128,1024]{1,0:T(8,128)(2,1)S(1)} collective-permute-done((bf16[128,1024]{1,0:T(8,128)(2,1)S(1)}, bf16[128,1024]{1,0:T(8,128)(2,1)S(1)}, u32[]{:S(2)}, u32[]{:S(2)}) %collective-permute-start.22) | collective-permute-done | bytes 262176 | tf_op jit(solution)/shard_map/ppermute | solution.py:30
  140.5 0.1 fusion.33
  140.6 5.1 %collective-permute-done.8 = bf16[128,1024]{1,0:T(8,128)(2,1)S(1)} collective-permute-done((bf16[128,1024]{1,0:T(8,128)(2,1)S(1)}, bf16[128,1024]{1,0:T(8,128)(2,1)S(1)}, u32[]{:S(2)}, u32[]{:S(2)}) %collective-permute-start.8) | collective-permute-done | bytes 262176 | tf_op jit(solution)/shard_map/ppermute | solution.py:30
  145.7 0.1 fusion.35
  145.8 3.4 %fusion.23 = bf16[256,1024]{1,0:T(8,128)(2,1)S(1)} fusion(bf16[256,1920]{1,0:T(8,128)(2,1)S(1)} %collective-permute-done.23.refs_3_, bf16[1024,7680]{1,0:T(8,128)(2,1)} %param.6, s32[]{:T(128)S(6)} %select_n.44), kind=kOutput, calls=%fused_computation.29 | convolution fusion | flops 1006895104 | bytes 5439492 | tf_op jit(solution)/shard_map/dot_general | solution.py:25
  149.2 1.6 collective-permute-start.24
  150.8 3.4 %fusion.29 = bf16[256,1024]{1,0:T(8,128)(2,1)S(1)} fusion(bf16[256,1920]{1,0:T(8,128)(2,1)S(1)} %collective-permute-done.9.refs_3_, bf16[1024,7680]{1,0:T(8,128)(2,1)} %param.7, s32[]{:T(128)S(6)} %select_n.44), kind=kOutput, calls=%fused_computation.31 | convolution fusion | flops 1006895104 | bytes 5439492 | tf_op jit(solution)/shard_map/dot_general | solution.py:25
  154.2 0.6 collective-permute-start.10
  154.8 5.1 %shard_map.76 = f32[1024,1920]{1,0:T(8,128)} custom-call(bf16[1024,256]{1,0:T(8,128)(2,1)S(1)} %get-tuple-element.7.refs_0_, bf16[1024,256]{1,0:T(8,128)(2,1)S(1)} %get-tuple-element.6.refs_1_, bf16[256,1920]{1,0:T(8,128)(2,1)S(1)} %get-tuple-element.5.refs_2_, bf16[256,1920]{1,0:T(8,128)(2,1)S(1)} %collective-permute-done.9.refs_3_), custom_call_target="tpu_custom_call" | custom-call | flops 2013265920 | bytes 10878976 | tf_op jit(solution)/shard_map/pallas_call | solution.py:111
  159.9 5.1 %shard_map.75 = f32[1024,1920]{1,0:T(8,128)} custom-call(bf16[1024,256]{1,0:T(8,128)(2,1)S(1)} %get-tuple-element.9.refs_0_, bf16[1024,256]{1,0:T(8,128)(2,1)S(1)} %get-tuple-element.8.refs_1_, bf16[256,1920]{1,0:T(8,128)(2,1)S(1)} %get-tuple-element.4.refs_2_, bf16[256,1920]{1,0:T(8,128)(2,1)S(1)} %collective-permute-done.23.refs_3_), custom_call_target="tpu_custom_call" | custom-call | flops 2013265920 | bytes 10878976 | tf_op jit(solution)/shard_map/pallas_call | solution.py:111
  165.0 0.1 fusion.32
  165.1 0.1 maximum_select_fusion.1
  165.3 2.0 %collective-permute-start.27 = (bf16[64,1024]{1,0:T(8,128)(2,1)S(1)}, bf16[64,1024]{1,0:T(8,128)(2,1)S(1)}, u32[]{:S(2)}, u32[]{:S(2)}) collective-permute-start(bf16[64,1024]{1,0:T(8,128)(2,1)S(1)} %get-tuple-element.11), channel_id=1, source_target_pairs={{0,8},{8,16},{16,24},{24,0},{1,9},{9,17},{17,25},{25,1},{2,10},{10... | collective-permute-start | bytes 393224 | tf_op jit(solution)/shard_map/ppermute | solution.py:44
  167.3 0.3 collective-permute-start.26
  167.6 0.1 fusion.34
  167.7 0.1 maximum_select_fusion
  167.9 2.1 %collective-permute-start.11 = (bf16[64,1024]{1,0:T(8,128)(2,1)S(1)}, bf16[64,1024]{1,0:T(8,128)(2,1)S(1)}, u32[]{:S(2)}, u32[]{:S(2)}) collective-permute-start(bf16[64,1024]{1,0:T(8,128)(2,1)S(1)} %get-tuple-element.17), channel_id=1, source_target_pairs={{0,24},{8,0},{16,8},{24,16},{1,25},{9,1},{17,9},{25,17},{2,26},{10... | collective-permute-start | bytes 393224 | tf_op jit(solution)/shard_map/ppermute | solution.py:44
  170.0 0.1 collective-permute-start.13
  170.1 5.4 %collective-permute-done.25 = bf16[64,1024]{1,0:T(8,128)(2,1)S(1)} collective-permute-done((bf16[64,1024]{1,0:T(8,128)(2,1)S(1)}, bf16[64,1024]{1,0:T(8,128)(2,1)S(1)}, u32[]{:S(2)}, u32[]{:S(2)}) %collective-permute-start.25) | collective-permute-done | bytes 131104 | tf_op jit(solution)/shard_map/ppermute | solution.py:44
  175.5 4.0 %collective-permute-done.26 = bf16[64,1024]{1,0:T(8,128)(2,1)S(1)} collective-permute-done((bf16[64,1024]{1,0:T(8,128)(2,1)S(1)}, bf16[64,1024]{1,0:T(8,128)(2,1)S(1)}, u32[]{:S(2)}, u32[]{:S(2)}) %collective-permute-start.26) | collective-permute-done | bytes 131104 | tf_op jit(solution)/shard_map/ppermute | solution.py:44
  179.5 0.7 add_convert_fusion
  180.3 0.2 collective-permute-done.11
  180.5 1.9 %collective-permute-done.13 = bf16[64,1024]{1,0:T(8,128)(2,1)S(1)} collective-permute-done((bf16[64,1024]{1,0:T(8,128)(2,1)S(1)}, bf16[64,1024]{1,0:T(8,128)(2,1)S(1)}, u32[]{:S(2)}, u32[]{:S(2)}) %collective-permute-start.13) | collective-permute-done | bytes 131104 | tf_op jit(solution)/shard_map/ppermute | solution.py:44
  182.5 6.3 %collective-permute-done.12 = bf16[64,1024]{1,0:T(8,128)(2,1)S(1)} collective-permute-done((bf16[64,1024]{1,0:T(8,128)(2,1)S(1)}, bf16[64,1024]{1,0:T(8,128)(2,1)S(1)}, u32[]{:S(2)}, u32[]{:S(2)}) %collective-permute-start.12) | collective-permute-done | bytes 131104 | tf_op jit(solution)/shard_map/ppermute | solution.py:44
  188.8 0.7 add_convert_fusion.1
  (26 shorter events, 0.5 us)
Async XLA Ops:
  1.9 11.9 %collective-permute-start.4 = (bf16[64,1024]{0,1:T(8,128)(2,1)S(1)}, bf16[64,1024]{0,1:T(8,128)(2,1)S(1)}, u32[]{:S(2)}, u32[]{:S(2)}) collective-permute-start(bf16[64,1024]{0,1:T(8,128)(2,1)S(1)} %copy.12), channel_id=1, source_target_pairs={{0,24},{8,0},{16,8},{24,16},{1,25},{9,1},{17,9},{25,17},{2,26},{10... | collective-permute-start | bytes 393224 | tf_op jit(solution)/shard_map/ppermute | solution.py:44
  7.1 22.3 %collective-permute-start.2 = (bf16[64,1024]{0,1:T(8,128)(2,1)S(1)}, bf16[64,1024]{0,1:T(8,128)(2,1)S(1)}, u32[]{:S(2)}, u32[]{:S(2)}) collective-permute-start(bf16[64,1024]{0,1:T(8,128)(2,1)S(1)} %copy.12), channel_id=1, source_target_pairs={{0,16},{8,24},{16,0},{24,8},{1,17},{9,25},{17,1},{25,9},{2,18},{10... | collective-permute-start | bytes 393224 | tf_op jit(solution)/shard_map/ppermute | solution.py:44
  7.1 23.8 %collective-permute-start = (bf16[64,1024]{0,1:T(8,128)(2,1)S(1)}, bf16[64,1024]{0,1:T(8,128)(2,1)S(1)}, u32[]{:S(2)}, u32[]{:S(2)}) collective-permute-start(bf16[64,1024]{0,1:T(8,128)(2,1)S(1)} %copy.12), channel_id=1, source_target_pairs={{0,8},{8,16},{16,24},{24,0},{1,9},{9,17},{17,25},{25,1},{2,10},{10... | collective-permute-start | bytes 393224 | tf_op jit(solution)/shard_map/ppermute | solution.py:44
  13.8 20.4 %collective-permute-start.5 = (bf16[64,1024]{0,1:T(8,128)(2,1)S(1)}, bf16[64,1024]{0,1:T(8,128)(2,1)}, u32[]{:S(2)}, u32[]{:S(2)}) collective-permute-start(bf16[64,1024]{0,1:T(8,128)(2,1)S(1)} %collective-permute-done.4), channel_id=1, source_target_pairs={{0,1},{1,0},{2,3},{3,2},{4,5},{5,4},{6,7},{7,6},{8,9},{9,8},{10,11... | collective-permute-start | bytes 393224 | tf_op jit(solution)/shard_map/ppermute | solution.py:30
  29.4 9.3 %collective-permute-start.3 = (bf16[64,1024]{0,1:T(8,128)(2,1)S(1)}, bf16[64,1024]{0,1:T(8,128)(2,1)}, u32[]{:S(2)}, u32[]{:S(2)}) collective-permute-start(bf16[64,1024]{0,1:T(8,128)(2,1)S(1)} %collective-permute-done.2), channel_id=1, source_target_pairs={{0,1},{1,0},{2,3},{3,2},{4,5},{5,4},{6,7},{7,6},{8,9},{9,8},{10,11... | collective-permute-start | bytes 393224 | tf_op jit(solution)/shard_map/ppermute | solution.py:30
  30.9 11.4 %collective-permute-start.1 = (bf16[64,1024]{0,1:T(8,128)(2,1)S(1)}, bf16[64,1024]{0,1:T(8,128)(2,1)}, u32[]{:S(2)}, u32[]{:S(2)}) collective-permute-start(bf16[64,1024]{0,1:T(8,128)(2,1)S(1)} %collective-permute-done), channel_id=1, source_target_pairs={{0,1},{1,0},{2,3},{3,2},{4,5},{5,4},{6,7},{7,6},{8,9},{9,8},{10,11... | collective-permute-start | bytes 393224 | tf_op jit(solution)/shard_map/ppermute | solution.py:30
  31.6 17.5 %collective-permute-start.18 = (bf16[64,1024]{0,1:T(8,128)(2,1)S(1)}, bf16[64,1024]{0,1:T(8,128)(2,1)S(1)}, u32[]{:S(2)}, u32[]{:S(2)}) collective-permute-start(bf16[64,1024]{0,1:T(8,128)(2,1)S(1)} %copy.14), channel_id=1, source_target_pairs={{0,24},{8,0},{16,8},{24,16},{1,25},{9,1},{17,9},{25,17},{2,26},{10... | collective-permute-start | bytes 393224 | tf_op jit(solution)/shard_map/ppermute | solution.py:44
  31.7 24.6 %collective-permute-start.16 = (bf16[64,1024]{0,1:T(8,128)(2,1)S(1)}, bf16[64,1024]{0,1:T(8,128)(2,1)S(1)}, u32[]{:S(2)}, u32[]{:S(2)}) collective-permute-start(bf16[64,1024]{0,1:T(8,128)(2,1)S(1)} %copy.14), channel_id=1, source_target_pairs={{0,16},{8,24},{16,0},{24,8},{1,17},{9,25},{17,1},{25,9},{2,18},{10... | collective-permute-start | bytes 393224 | tf_op jit(solution)/shard_map/ppermute | solution.py:44
  34.2 22.6 %collective-permute-start.14 = (bf16[64,1024]{0,1:T(8,128)(2,1)S(1)}, bf16[64,1024]{0,1:T(8,128)(2,1)}, u32[]{:S(2)}, u32[]{:S(2)}) collective-permute-start(bf16[64,1024]{0,1:T(8,128)(2,1)S(1)} %copy.14), channel_id=1, source_target_pairs={{0,8},{8,16},{16,24},{24,0},{1,9},{9,17},{17,25},{25,1},{2,10},{10... | collective-permute-start | bytes 393224 | tf_op jit(solution)/shard_map/ppermute | solution.py:44
  49.1 26.9 %collective-permute-start.6 = (bf16[256,1920]{1,0:T(8,128)(2,1)}, bf16[256,1920]{1,0:T(8,128)(2,1)}, u32[]{:S(2)}, u32[]{:S(2)}) collective-permute-start(bf16[256,1920]{1,0:T(8,128)(2,1)} %convolution_convert_fusion.1), channel_id=1, source_target_pairs={{0,2},{2,0},{4,6},{6,4},{1,3},{3,1},{5,7},{7,5},{8,10},{10,8},{12,... | collective-permute-start | bytes 2949128 | tf_op jit(solution)/shard_map/ppermute | solution.py:30
  49.1 9.4 %collective-permute-start.19 = (bf16[64,1024]{0,1:T(8,128)(2,1)S(1)}, bf16[64,1024]{0,1:T(8,128)(2,1)S(1)}, u32[]{:S(2)}, u32[]{:S(2)}) collective-permute-start(bf16[64,1024]{0,1:T(8,128)(2,1)S(1)} %collective-permute-done.18), channel_id=1, source_target_pairs={{0,1},{1,0},{2,3},{3,2},{4,5},{5,4},{6,7},{7,6},{8,9},{9,8},{10,11... | collective-permute-start | bytes 393224 | tf_op jit(solution)/shard_map/ppermute | solution.py:30
  56.3 9.3 %collective-permute-start.17 = (bf16[64,1024]{0,1:T(8,128)(2,1)S(1)}, bf16[64,1024]{0,1:T(8,128)(2,1)}, u32[]{:S(2)}, u32[]{:S(2)}) collective-permute-start(bf16[64,1024]{0,1:T(8,128)(2,1)S(1)} %collective-permute-done.16), channel_id=1, source_target_pairs={{0,1},{1,0},{2,3},{3,2},{4,5},{5,4},{6,7},{7,6},{8,9},{9,8},{10,11... | collective-permute-start | bytes 393224 | tf_op jit(solution)/shard_map/ppermute | solution.py:30
  56.8 12.4 %collective-permute-start.15 = (bf16[64,1024]{0,1:T(8,128)(2,1)}, bf16[64,1024]{0,1:T(8,128)(2,1)}, u32[]{:S(2)}, u32[]{:S(2)}) collective-permute-start(bf16[64,1024]{0,1:T(8,128)(2,1)} %collective-permute-done.14), channel_id=1, source_target_pairs={{0,1},{1,0},{2,3},{3,2},{4,5},{5,4},{6,7},{7,6},{8,9},{9,8},{10,11... | collective-permute-start | bytes 393224 | tf_op jit(solution)/shard_map/ppermute | solution.py:30
  76.0 5.2 %collective-permute-start.20 = (bf16[256,1920]{1,0:T(8,128)(2,1)}, bf16[256,1920]{1,0:T(8,128)(2,1)}, u32[]{:S(2)}, u32[]{:S(2)}) collective-permute-start(bf16[256,1920]{1,0:T(8,128)(2,1)} %convolution_convert_fusion), channel_id=1, source_target_pairs={{0,2},{2,0},{4,6},{6,4},{1,3},{3,1},{5,7},{7,5},{8,10},{10,8},{12,... | collective-permute-start | bytes 2949128 | tf_op jit(solution)/shard_map/ppermute | solution.py:30
  79.7 24.8 %collective-permute-start.7 = (bf16[256,1920]{1,0:T(8,128)(2,1)S(1)}, bf16[256,1920]{1,0:T(8,128)(2,1)}, u32[]{:S(2)}, u32[]{:S(2)}) collective-permute-start(bf16[256,1920]{1,0:T(8,128)(2,1)S(1)} %fusion), channel_id=1, source_target_pairs={{0,4},{2,6},{4,0},{6,2},{1,5},{3,7},{5,1},{7,3},{8,12},{10,14},{12... | collective-permute-start | bytes 2949128 | tf_op jit(solution)/shard_map/ppermute | solution.py:30
  85.8 39.3 %collective-permute-start.21 = (bf16[256,1920]{1,0:T(8,128)(2,1)}, bf16[256,1920]{1,0:T(8,128)(2,1)}, u32[]{:S(2)}, u32[]{:S(2)}) collective-permute-start(bf16[256,1920]{1,0:T(8,128)(2,1)} %fusion.1), channel_id=1, source_target_pairs={{0,4},{2,6},{4,0},{6,2},{1,5},{3,7},{5,1},{7,3},{8,12},{10,14},{12... | collective-permute-start | bytes 2949128 | tf_op jit(solution)/shard_map/ppermute | solution.py:30
  131.2 14.6 %collective-permute-start.23 = (bf16[256,1920]{1,0:T(8,128)(2,1)S(1)}, bf16[256,1920]{1,0:T(8,128)(2,1)S(1)}, u32[]{:S(2)}, u32[]{:S(2)}) collective-permute-start(bf16[256,1920]{1,0:T(8,128)(2,1)S(1)} %get-tuple-element.4.refs_2_), channel_id=1, source_target_pairs={{0,2},{2,0},{4,6},{6,4},{1,3},{3,1},{5,7},{7,5},{8,10},{10,8},{12,... | collective-permute-start | bytes 2949128 | tf_op jit(solution)/shard_map/ppermute | solution.py:30
  131.3 9.2 %collective-permute-start.22 = (bf16[128,1024]{1,0:T(8,128)(2,1)S(1)}, bf16[128,1024]{1,0:T(8,128)(2,1)S(1)}, u32[]{:S(2)}, u32[]{:S(2)}) collective-permute-start(bf16[128,1024]{1,0:T(8,128)(2,1)S(1)} %bitcast.38), channel_id=1, source_target_pairs={{0,1},{1,0},{2,3},{3,2},{4,5},{5,4},{6,7},{7,6},{8,9},{9,8},{10,11... | collective-permute-start | bytes 786440 | tf_op jit(solution)/shard_map/ppermute | solution.py:30
  136.3 9.4 %collective-permute-start.8 = (bf16[128,1024]{1,0:T(8,128)(2,1)S(1)}, bf16[128,1024]{1,0:T(8,128)(2,1)S(1)}, u32[]{:S(2)}, u32[]{:S(2)}) collective-permute-start(bf16[128,1024]{1,0:T(8,128)(2,1)S(1)} %bitcast.39), channel_id=1, source_target_pairs={{0,1},{1,0},{2,3},{3,2},{4,5},{5,4},{6,7},{7,6},{8,9},{9,8},{10,11... | collective-permute-start | bytes 786440 | tf_op jit(solution)/shard_map/ppermute | solution.py:30
  136.9 13.8 %collective-permute-start.9 = (bf16[256,1920]{1,0:T(8,128)(2,1)S(1)}, bf16[256,1920]{1,0:T(8,128)(2,1)S(1)}, u32[]{:S(2)}, u32[]{:S(2)}) collective-permute-start(bf16[256,1920]{1,0:T(8,128)(2,1)S(1)} %get-tuple-element.5.refs_2_), channel_id=1, source_target_pairs={{0,2},{2,0},{4,6},{6,4},{1,3},{3,1},{5,7},{7,5},{8,10},{10,8},{12,... | collective-permute-start | bytes 2949128 | tf_op jit(solution)/shard_map/ppermute | solution.py:30
  149.2 15.8 %collective-permute-start.24 = (bf16[128,1024]{1,0:T(8,128)(2,1)S(1)}, bf16[128,1024]{1,0:T(8,128)(2,1)S(1)}, u32[]{:S(2)}, u32[]{:S(2)}) collective-permute-start(bf16[128,1024]{1,0:T(8,128)(2,1)S(1)} %bitcast.37), channel_id=1, source_target_pairs={{0,1},{1,0},{2,3},{3,2},{4,5},{5,4},{6,7},{7,6},{8,9},{9,8},{10,11... | collective-permute-start | bytes 786440 | tf_op jit(solution)/shard_map/ppermute | solution.py:30
  154.2 13.4 %collective-permute-start.10 = (bf16[128,1024]{1,0:T(8,128)(2,1)S(1)}, bf16[128,1024]{1,0:T(8,128)(2,1)S(1)}, u32[]{:S(2)}, u32[]{:S(2)}) collective-permute-start(bf16[128,1024]{1,0:T(8,128)(2,1)S(1)} %bitcast.36), channel_id=1, source_target_pairs={{0,1},{1,0},{2,3},{3,2},{4,5},{5,4},{6,7},{7,6},{8,9},{9,8},{10,11... | collective-permute-start | bytes 786440 | tf_op jit(solution)/shard_map/ppermute | solution.py:30
  165.2 10.3 %collective-permute-start.25 = (bf16[64,1024]{1,0:T(8,128)(2,1)S(1)}, bf16[64,1024]{1,0:T(8,128)(2,1)S(1)}, u32[]{:S(2)}, u32[]{:S(2)}) collective-permute-start(bf16[64,1024]{1,0:T(8,128)(2,1)S(1)} %get-tuple-element.10), channel_id=1, source_target_pairs={{0,24},{8,0},{16,8},{24,16},{1,25},{9,1},{17,9},{25,17},{2,26},{10... | collective-permute-start | bytes 393224 | tf_op jit(solution)/shard_map/ppermute | solution.py:44
  165.3 10.2 %collective-permute-start.27 = (bf16[64,1024]{1,0:T(8,128)(2,1)S(1)}, bf16[64,1024]{1,0:T(8,128)(2,1)S(1)}, u32[]{:S(2)}, u32[]{:S(2)}) collective-permute-start(bf16[64,1024]{1,0:T(8,128)(2,1)S(1)} %get-tuple-element.11), channel_id=1, source_target_pairs={{0,8},{8,16},{16,24},{24,0},{1,9},{9,17},{17,25},{25,1},{2,10},{10... | collective-permute-start | bytes 393224 | tf_op jit(solution)/shard_map/ppermute | solution.py:44
  167.3 12.2 %collective-permute-start.26 = (bf16[64,1024]{1,0:T(8,128)(2,1)S(1)}, bf16[64,1024]{1,0:T(8,128)(2,1)S(1)}, u32[]{:S(2)}, u32[]{:S(2)}) collective-permute-start(bf16[64,1024]{1,0:T(8,128)(2,1)S(1)} %get-tuple-element.12), channel_id=1, source_target_pairs={{0,16},{8,24},{16,0},{24,8},{1,17},{9,25},{17,1},{25,9},{2,18},{10... | collective-permute-start | bytes 393224 | tf_op jit(solution)/shard_map/ppermute | solution.py:44
  167.9 12.6 %collective-permute-start.11 = (bf16[64,1024]{1,0:T(8,128)(2,1)S(1)}, bf16[64,1024]{1,0:T(8,128)(2,1)S(1)}, u32[]{:S(2)}, u32[]{:S(2)}) collective-permute-start(bf16[64,1024]{1,0:T(8,128)(2,1)S(1)} %get-tuple-element.17), channel_id=1, source_target_pairs={{0,24},{8,0},{16,8},{24,16},{1,25},{9,1},{17,9},{25,17},{2,26},{10... | collective-permute-start | bytes 393224 | tf_op jit(solution)/shard_map/ppermute | solution.py:44
  170.0 12.4 %collective-permute-start.13 = (bf16[64,1024]{1,0:T(8,128)(2,1)S(1)}, bf16[64,1024]{1,0:T(8,128)(2,1)S(1)}, u32[]{:S(2)}, u32[]{:S(2)}) collective-permute-start(bf16[64,1024]{1,0:T(8,128)(2,1)S(1)} %get-tuple-element.18), channel_id=1, source_target_pairs={{0,8},{8,16},{16,24},{24,0},{1,9},{9,17},{17,25},{25,1},{2,10},{10... | collective-permute-start | bytes 393224 | tf_op jit(solution)/shard_map/ppermute | solution.py:44
  175.5 13.3 %collective-permute-start.12 = (bf16[64,1024]{1,0:T(8,128)(2,1)S(1)}, bf16[64,1024]{1,0:T(8,128)(2,1)S(1)}, u32[]{:S(2)}, u32[]{:S(2)}) collective-permute-start(bf16[64,1024]{1,0:T(8,128)(2,1)S(1)} %get-tuple-element.19), channel_id=1, source_target_pairs={{0,16},{8,24},{16,0},{24,8},{1,17},{9,25},{17,1},{25,9},{2,18},{10... | collective-permute-start | bytes 393224 | tf_op jit(solution)/shard_map/ppermute | solution.py:44

commit v2 on v1

--- a/solution.py
+++ b/solution.py
@@ -4,6 +4,7 @@
 from jax.experimental import pallas as pl
 from jax.experimental.pallas import tpu as pltpu
 from jax.sharding import PartitionSpec as P
+
 
 root_half = 0.7071067811865476
 inv_root_tau = 0.3989422804014327
@@ -35,10 +36,6 @@
     return lax.dynamic_slice_in_dim(values, which * half, half, 0)
 
 
-def after(values, earlier):
-    return lax.optimization_barrier((values, earlier[:8, :128]))[0]
-
-
 def shift(values, by):
     n = lax.axis_size("dp")
     return lax.ppermute(values, "dp", [(i, (i + by) % n) for i in range(n)])
@@ -51,10 +48,12 @@
         side = lax.axis_index("col")
         first = lax.dynamic_slice_in_dim(values, side * kept, kept, 0)
         second = lax.dynamic_slice_in_dim(values, (1 - side) * kept, kept, 0)
+        moved = [shift(first, by) for by in range(1, groups)]
+        moved = jnp.concatenate(moved)
+        swapped = swap(moved, "col", 1)
         rows = [first, second]
-        moved = [shift(first, by) for by in range(1, groups)]
-        for part in moved:
-            rows += [part, swap(part, "col", 1)]
+        for i in range(groups - 1):
+            rows += [moved[i * kept : (i + 1) * kept], swapped[i * kept : (i + 1) * kept]]
         return jnp.concatenate(rows)
     gathered = lax.all_gather(values, "dp", axis=0, tiled=False)
     order = (lax.axis_index("dp") - jnp.arange(groups)) % groups
@@ -138,13 +137,12 @@
     hidden_part = core_sum(token_mine, token_others, up)
     hidden = row_total(hidden_part)
 
-    cotangent = after(cotangent, hidden_part)
     cot_mine, cot_others = take_half(cotangent, side), take_half(cotangent, 1 - side)
     grad_part = core_sum(cot_mine, cot_others, down)
     grad = row_total(grad_part)
 
     active_val, slope_val = gelu_pair(hidden)
-    active = active_val.astype(BF16)
+    active, slope_val = lax.optimization_barrier((active_val.astype(BF16), slope_val))
     active_other = swap(active, "row", 1)
     output_mine = column_sum(active, down)
     output_others = column_sum(active_other, down)

time: 190 us -> 184 us (0.968)
  starting transfers between devices: 28.8 us -> 24.3 us
  waiting for transfers between devices: 107 us -> 103 us
  local copies, waits for them, and re-layouts: 7.02 us -> 9.08 us
    ppermute x16 -> x12, waiting for transfers between devices: 64 us -> 58.1 us  [swap(): return lax.ppermute(values, axis, [(i, i ^ bit) for i in range(n)])]
    ppermute x16 -> x12, starting transfers between devices: 13.6 us -> 7.7 us  [swap(): return lax.ppermute(values, axis, [(i, i ^ bit) for i in range(n)])]
    convert_element_type x1, other arithmetic: 2.65 us -> 0.31 us  [shards(): hidden_grad = (grad * slope_val).astype(BF16)]
    add x0 -> x1, other arithmetic: none -> 2.19 us  [gelu_pair(): return (hidden * normal_cdf, normal_cdf + hidden * density)]
    slice x0 -> x2, local copies, waits for them, and re-layouts: none -> 2.06 us  [gather_tokens(): rows += [moved[i * kept:(i + 1) * kept], swapped[i * kept:(i + 1) * kept]]]
  transfers between devices with their start and end apart: 28 -> 24, of which waited for: 16 -> 11; matrix products, arithmetic and copies ran while one was open for 18% -> 23% of each run, Pallas kernels for 5% -> 6%
where the time goes in v2:
time: 184 us; the launch traced here: 183 us
  waiting for transfers between devices  103 us (56%)
  matrix products  29.8 us (16%)
  starting transfers between devices  24.3 us (13%)
  Pallas kernels  10.2 us (6%)
  local copies, waits for them, and re-layouts  9.08 us (5%)
  other arithmetic  5.84 us (3%)
    ppermute x12, waiting for transfers between devices, swap(): return lax.ppermute(values, axis, [(i, i ^ bit) for i in range(n)])  58.1 us
    ppermute x12, waiting for transfers between devices, shift(): return lax.ppermute(values, 'dp', [(i, (i + by) % n) for i in range(n)])  44.8 us
    ppermute x12, starting transfers between devices, shift(): return lax.ppermute(values, 'dp', [(i, (i + by) % n) for i in range(n)])  16.6 us
    dot_general x4, matrix products, dot(): return jnp.dot(left, right, preferred_element_type=F32)  16.1 us
    dot_general x4, matrix products, dot_across(): lax.dot_general(left, right, (((1,), (1,)), ((), ())), preferred_element_...  13.7 us
    pallas_call x2, Pallas kernels, weight_gradient(): pl.pallas_call(lambda *refs: gradient_kernel(factor, *refs), out_shape=ja...  10.2 us
    ppermute x12, starting transfers between devices, swap(): return lax.ppermute(values, axis, [(i, i ^ bit) for i in range(n)])  7.7 us
    concatenate x2, local copies, waits for them, and re-layouts, gather_tokens(): return jnp.concatenate(rows)  4.88 us
  transfers between devices with their start and end apart: 24, of which 11 were waited for; matrix products, arithmetic and copies ran while one was open for 23% of the time, Pallas kernels for 6%

profile of v2, /device:TPU:0, one launch (start us, length us, event | category | flops | bytes accessed | tf_op | source)
XLA Modules:
  0.0 182.9 jit_solution(195254968584276228)
XLA Ops:
  0.6 1.1 constant_dynamic-slice_fusion
  1.8 0.2 copy.12
  2.0 5.1 %collective-permute-start.2 = (bf16[64,1024]{0,1:T(8,128)(2,1)S(1)}, bf16[64,1024]{0,1:T(8,128)(2,1)S(1)}, u32[]{:S(2)}, u32[]{:S(2)}) collective-permute-start(bf16[64,1024]{0,1:T(8,128)(2,1)S(1)} %copy.12), channel_id=1, source_target_pairs={{0,24},{8,0},{16,8},{24,16},{1,25},{9,1},{17,9},{25,17},{2,26},{10... | collective-permute-start | bytes 393224 | tf_op jit(solution)/shard_map/ppermute | solution.py:41
  7.1 1.0 collective-permute-start
  8.1 5.7 %collective-permute-done.2 = bf16[64,1024]{0,1:T(8,128)(2,1)S(1)} collective-permute-done((bf16[64,1024]{0,1:T(8,128)(2,1)S(1)}, bf16[64,1024]{0,1:T(8,128)(2,1)S(1)}, u32[]{:S(2)}, u32[]{:S(2)}) %collective-permute-start.2) | collective-permute-done | bytes 131104 | tf_op jit(solution)/shard_map/ppermute | solution.py:41
  13.8 15.6 %collective-permute-done.1 = bf16[64,1024]{0,1:T(8,128)(2,1)S(1)} collective-permute-done((bf16[64,1024]{0,1:T(8,128)(2,1)S(1)}, bf16[64,1024]{0,1:T(8,128)(2,1)S(1)}, u32[]{:S(2)}, u32[]{:S(2)}) %collective-permute-start.1) | collective-permute-done | bytes 131104 | tf_op jit(solution)/shard_map/ppermute | solution.py:41
  29.4 1.0 pad_maximum_fusion
  30.4 1.5 collective-permute-start.3
  32.0 0.2 copy.14
  32.1 0.1 collective-permute-start.14
  32.2 2.9 %collective-permute-start.13 = (bf16[64,1024]{0,1:T(8,128)(2,1)S(1)}, bf16[64,1024]{0,1:T(8,128)(2,1)S(1)}, u32[]{:S(2)}, u32[]{:S(2)}) collective-permute-start(bf16[64,1024]{0,1:T(8,128)(2,1)S(1)} %copy.14), channel_id=1, source_target_pairs={{0,16},{8,24},{16,0},{24,8},{1,17},{9,25},{17,1},{25,9},{2,18},{10... | collective-permute-start | bytes 393224 | tf_op jit(solution)/shard_map/ppermute | solution.py:41
  35.1 1.9 %collective-permute-start.12 = (bf16[64,1024]{0,1:T(8,128)(2,1)S(1)}, bf16[64,1024]{0,1:T(8,128)(2,1)S(1)}, u32[]{:S(2)}, u32[]{:S(2)}) collective-permute-start(bf16[64,1024]{0,1:T(8,128)(2,1)S(1)} %copy.14), channel_id=1, source_target_pairs={{0,8},{8,16},{16,24},{24,0},{1,9},{9,17},{17,25},{25,1},{2,10},{10... | collective-permute-start | bytes 393224 | tf_op jit(solution)/shard_map/ppermute | solution.py:41
  37.0 0.2 copy.13
  37.2 6.3 %collective-permute-done.3 = bf16[192,1024]{0,1:T(8,128)(2,1)S(1)} collective-permute-done((bf16[192,1024]{0,1:T(8,128)(2,1)}, bf16[192,1024]{0,1:T(8,128)(2,1)S(1)}, u32[]{:S(2)}, u32[]{:S(2)}) %collective-permute-start.3) | collective-permute-done | bytes 393248 | tf_op jit(solution)/shard_map/ppermute | solution.py:31
  43.5 1.0 fusion.53
  44.5 2.4 %concatenate.25 = bf16[512,1024]{0,1:T(8,128)(2,1)S(1)} concatenate(bf16[64,1024]{0,1:T(8,128)(2,1)S(1)} %copy.12, bf16[64,1024]{0,1:T(8,128)(2,1)S(1)} %copy.13, bf16[64,1024]{0,1:T(8,128)(2,1)S(1)} %collective-permute-done, bf16[64,1024]{0,1:T(8,128)(2,1)} %get-tuple-element.33, bf16[64,1024]{0,1:T(8,128)(2,1)S(1)} %collective-permute-done.1, ...), dimensions={0} | concatenate | bytes 2097152 | tf_op jit(solution)/shard_map/concatenate | solution.py:57
  46.9 4.4 %convolution_convert_fusion.1 = bf16[256,1920]{1,0:T(8,128)(2,1)} fusion(bf16[1024,7680]{1,0:T(8,128)(2,1)} %param.6, s32[]{:T(128)S(6)} %select_n.44, bf16[512,1024]{0,1:T(8,128)(2,1)S(1)} %concatenate.25, s32[]{:T(128)S(6)} %select_n.45), kind=kOutput, calls=%fused_computation.4 | convolution fusion | flops 1007124480 | bytes 5439496 | tf_op jit(solution)/shard_map/dot_general | solution.py:22
  51.3 6.0 %collective-permute-done.13 = bf16[64,1024]{0,1:T(8,128)(2,1)S(1)} collective-permute-done((bf16[64,1024]{0,1:T(8,128)(2,1)S(1)}, bf16[64,1024]{0,1:T(8,128)(2,1)S(1)}, u32[]{:S(2)}, u32[]{:S(2)}) %collective-permute-start.13) | collective-permute-done | bytes 131104 | tf_op jit(solution)/shard_map/ppermute | solution.py:41
  57.3 0.3 pad_maximum_fusion.1
  57.6 0.6 collective-permute-start.15
  58.1 0.2 copy.15
  58.3 11.6 %collective-permute-done.15 = bf16[192,1024]{0,1:T(8,128)(2,1)S(1)} collective-permute-done((bf16[192,1024]{0,1:T(8,128)(2,1)S(1)}, bf16[192,1024]{0,1:T(8,128)(2,1)S(1)}, u32[]{:S(2)}, u32[]{:S(2)}) %collective-permute-start.15) | collective-permute-done | bytes 393248 | tf_op jit(solution)/shard_map/ppermute | solution.py:31
  69.9 1.0 fusion.49
  70.9 2.4 %concatenate.29 = bf16[512,1024]{0,1:T(8,128)(2,1)S(1)} concatenate(bf16[64,1024]{0,1:T(8,128)(2,1)S(1)} %copy.14, bf16[64,1024]{0,1:T(8,128)(2,1)S(1)} %copy.15, bf16[64,1024]{0,1:T(8,128)(2,1)S(1)} %collective-permute-done.12, bf16[64,1024]{0,1:T(8,128)(2,1)} %get-tuple-element.23, bf16[64,1024]{0,1:T(8,128)(2,1)S(1)} %collective-permute-done.13, ...), dimensions={0} | concatenate | bytes 2097152 | tf_op jit(solution)/shard_map/concatenate | solution.py:57
  73.4 4.4 %convolution_convert_fusion = bf16[256,1920]{1,0:T(8,128)(2,1)} fusion(bf16[1024,7680]{1,0:T(8,128)(2,1)} %param.7, s32[]{:T(128)S(6)} %select_n.44, bf16[512,1024]{0,1:T(8,128)(2,1)S(1)} %concatenate.29, s32[]{:T(128)S(6)} %select_n.45), kind=kOutput, calls=%fused_computation.3 | convolution fusion | flops 1007124480 | bytes 5439496 | tf_op jit(solution)/shard_map/dot_general | solution.py:22
  77.8 3.7 %fusion = bf16[256,1920]{1,0:T(8,128)(2,1)S(1)} fusion(bf16[1024,7680]{1,0:T(8,128)(2,1)} %param.6, s32[]{:T(128)S(6)} %select_n.44, bf16[256,1920]{1,0:T(8,128)(2,1)} %collective-permute-done.4, bf16[512,1024]{0,1:T(8,128)(2,1)S(1)} %concatenate.25, s32[]{:T(128)S(6)} %select_n.43), kind=kOutput, calls=%fused_computation.5 | convolution fusion | flops 1008107520 | bytes 6422536 | tf_op jit(solution)/shard_map/dot_general | solution.py:22
  81.4 1.6 collective-permute-start.5
  83.0 0.1 dynamic-slice_bitcast_fusion.2
  83.1 3.7 %fusion.1 = bf16[256,1920]{1,0:T(8,128)(2,1)S(1)} fusion(bf16[1024,7680]{1,0:T(8,128)(2,1)} %param.7, s32[]{:T(128)S(6)} %select_n.44, bf16[256,1920]{1,0:T(8,128)(2,1)} %collective-permute-done.16, bf16[512,1024]{0,1:T(8,128)(2,1)S(1)} %concatenate.29, s32[]{:T(128)S(6)} %select_n.43), kind=kOutput, calls=%fused_computation.6 | convolution fusion | flops 1008107520 | bytes 6422536 | tf_op jit(solution)/shard_map/dot_general | solution.py:22
  86.7 0.6 collective-permute-start.17
  87.3 18.9 %collective-permute-done.5 = bf16[256,1920]{1,0:T(8,128)(2,1)} collective-permute-done((bf16[256,1920]{1,0:T(8,128)(2,1)S(1)}, bf16[256,1920]{1,0:T(8,128)(2,1)}, u32[]{:S(2)}, u32[]{:S(2)}) %collective-permute-start.5) | collective-permute-done | bytes 983072 | tf_op jit(solution)/shard_map/ppermute | solution.py:31
  106.2 2.2 %fusion.17 = (f32[256,1920]{1,0:T(8,128)S(1)}, bf16[256,1920]{1,0:T(8,128)(2,1)S(1)}) fusion(bf16[256,1920]{1,0:T(8,128)(2,1)} %collective-permute-done.5, bf16[256,1920]{1,0:T(8,128)(2,1)S(1)} %fusion), kind=kLoop, calls=%fused_computation.22 | loop fusion | flops 6389760 | bytes 4915200 | tf_op jit(solution)/shard_map/add | solution.py:18
  108.4 0.1 collective-permute-start.7
  108.5 3.4 %fusion.24 = bf16[256,1024]{1,0:T(8,128)(2,1)S(1)} fusion(bf16[256,1920]{1,0:T(8,128)(2,1)S(1)} %get-tuple-element.6.refs_2_, bf16[1024,7680]{1,0:T(8,128)(2,1)} %param.7, s32[]{:T(128)S(6)} %select_n.44), kind=kOutput, calls=%fused_computation.29 | convolution fusion | flops 1006895104 | bytes 5439492 | tf_op jit(solution)/shard_map/dot_general | solution.py:26
  112.0 0.6 collective-permute-start.6
  112.5 14.2 %collective-permute-done.17 = bf16[256,1920]{1,0:T(8,128)(2,1)S(1)} collective-permute-done((bf16[256,1920]{1,0:T(8,128)(2,1)S(1)}, bf16[256,1920]{1,0:T(8,128)(2,1)S(1)}, u32[]{:S(2)}, u32[]{:S(2)}) %collective-permute-start.17) | collective-permute-done | bytes 983072 | tf_op jit(solution)/shard_map/ppermute | solution.py:31
  126.8 0.3 multiply_convert_fusion.refs_2_
  127.1 3.4 %fusion.18 = bf16[256,1024]{1,0:T(8,128)(2,1)S(1)} fusion(bf16[256,1920]{1,0:T(8,128)(2,1)S(1)} %multiply_convert_fusion.refs_2_, bf16[1024,7680]{1,0:T(8,128)(2,1)} %param.6, s32[]{:T(128)S(6)} %select_n.44), kind=kOutput, calls=%fused_computation.27 | convolution fusion | flops 1006895104 | bytes 5439492 | tf_op jit(solution)/shard_map/dot_general | solution.py:26
  130.5 0.6 collective-permute-start.18
  131.1 0.1 dynamic-slice_bitcast_fusion
  131.2 0.1 collective-permute-start.19
  131.3 0.1 fusion.33
  131.4 7.1 %collective-permute-done.18 = bf16[128,1024]{1,0:T(8,128)(2,1)S(1)} collective-permute-done((bf16[128,1024]{1,0:T(8,128)(2,1)S(1)}, bf16[128,1024]{1,0:T(8,128)(2,1)S(1)}, u32[]{:S(2)}, u32[]{:S(2)}) %collective-permute-start.18) | collective-permute-done | bytes 262176 | tf_op jit(solution)/shard_map/ppermute | solution.py:31
  138.5 0.1 fusion.31
  138.6 3.4 %fusion.27 = bf16[256,1024]{1,0:T(8,128)(2,1)S(1)} fusion(bf16[256,1920]{1,0:T(8,128)(2,1)S(1)} %collective-permute-done.7.refs_3_, bf16[1024,7680]{1,0:T(8,128)(2,1)} %param.7, s32[]{:T(128)S(6)} %select_n.44), kind=kOutput, calls=%fused_computation.30 | convolution fusion | flops 1006895104 | bytes 5439492 | tf_op jit(solution)/shard_map/dot_general | solution.py:26
  142.1 0.6 collective-permute-start.8
  142.6 3.4 %fusion.21 = bf16[256,1024]{1,0:T(8,128)(2,1)S(1)} fusion(bf16[256,1920]{1,0:T(8,128)(2,1)S(1)} %collective-permute-done.19.refs_3_, bf16[1024,7680]{1,0:T(8,128)(2,1)} %param.6, s32[]{:T(128)S(6)} %select_n.44), kind=kOutput, calls=%fused_computation.28 | convolution fusion | flops 1006895104 | bytes 5439492 | tf_op jit(solution)/shard_map/dot_general | solution.py:26
  146.1 1.6 collective-permute-start.20
  147.7 5.1 %shard_map.75 = f32[1024,1920]{1,0:T(8,128)} custom-call(bf16[1024,256]{1,0:T(8,128)(2,1)S(1)} %get-tuple-element.13.refs_0_, bf16[1024,256]{1,0:T(8,128)(2,1)S(1)} %get-tuple-element.12.refs_1_, bf16[256,1920]{1,0:T(8,128)(2,1)S(1)} %multiply_convert_fusion.refs_2_, bf16[256,1920]{1,0:T(8,128)(2,1)S(1)} %collective-permute-done.19.refs_3_), custom_call_target="tpu_custom_call" | custom-call | flops 2013265920 | bytes 10878976 | tf_op jit(solution)/shard_map/pallas_call | solution.py:110
  152.8 5.1 %shard_map.76 = f32[1024,1920]{1,0:T(8,128)} custom-call(bf16[1024,256]{1,0:T(8,128)(2,1)S(1)} %get-tuple-element.11.refs_0_, bf16[1024,256]{1,0:T(8,128)(2,1)S(1)} %get-tuple-element.10.refs_1_, bf16[256,1920]{1,0:T(8,128)(2,1)S(1)} %get-tuple-element.6.refs_2_, bf16[256,1920]{1,0:T(8,128)(2,1)S(1)} %collective-permute-done.7.refs_3_), custom_call_target="tpu_custom_call" | custom-call | flops 2013265920 | bytes 10878976 | tf_op jit(solution)/shard_map/pallas_call | solution.py:110
  157.9 0.1 fusion.32
  158.0 0.1 maximum_select_fusion
  158.2 0.1 collective-permute-start.9
  158.2 2.0 %collective-permute-start.11 = (bf16[64,1024]{1,0:T(8,128)(2,1)S(1)}, bf16[64,1024]{1,0:T(8,128)(2,1)S(1)}, u32[]{:S(2)}, u32[]{:S(2)}) collective-permute-start(bf16[64,1024]{1,0:T(8,128)(2,1)S(1)} %get-tuple-element.25), channel_id=1, source_target_pairs={{0,8},{8,16},{16,24},{24,0},{1,9},{9,17},{17,25},{25,1},{2,10},{10... | collective-permute-start | bytes 393224 | tf_op jit(solution)/shard_map/ppermute | solution.py:41
  160.2 1.4 collective-permute-start.10
  161.6 0.1 fusion.30
  161.7 0.1 maximum_select_fusion.1
  161.9 1.0 collective-permute-start.21
  162.9 1.0 collective-permute-start.23
  164.0 4.7 %collective-permute-done.9 = bf16[64,1024]{1,0:T(8,128)(2,1)S(1)} collective-permute-done((bf16[64,1024]{1,0:T(8,128)(2,1)S(1)}, bf16[64,1024]{1,0:T(8,128)(2,1)S(1)}, u32[]{:S(2)}, u32[]{:S(2)}) %collective-permute-start.9) | collective-permute-done | bytes 131104 | tf_op jit(solution)/shard_map/ppermute | solution.py:41
  168.7 9.1 %collective-permute-done.10 = bf16[64,1024]{1,0:T(8,128)(2,1)S(1)} collective-permute-done((bf16[64,1024]{1,0:T(8,128)(2,1)S(1)}, bf16[64,1024]{1,0:T(8,128)(2,1)S(1)}, u32[]{:S(2)}, u32[]{:S(2)}) %collective-permute-start.10) | collective-permute-done | bytes 131104 | tf_op jit(solution)/shard_map/ppermute | solution.py:41
  177.8 0.7 add_convert_fusion.1
  178.5 3.7 %collective-permute-done.22 = bf16[64,1024]{1,0:T(8,128)(2,1)S(1)} collective-permute-done((bf16[64,1024]{1,0:T(8,128)(2,1)S(1)}, bf16[64,1024]{1,0:T(8,128)(2,1)S(1)}, u32[]{:S(2)}, u32[]{:S(2)}) %collective-permute-start.22) | collective-permute-done | bytes 131104 | tf_op jit(solution)/shard_map/ppermute | solution.py:41
  182.2 0.7 add_convert_fusion
  (23 shorter events, 0.2 us)
Async XLA Ops:
  2.0 11.9 %collective-permute-start.2 = (bf16[64,1024]{0,1:T(8,128)(2,1)S(1)}, bf16[64,1024]{0,1:T(8,128)(2,1)S(1)}, u32[]{:S(2)}, u32[]{:S(2)}) collective-permute-start(bf16[64,1024]{0,1:T(8,128)(2,1)S(1)} %copy.12), channel_id=1, source_target_pairs={{0,24},{8,0},{16,8},{24,16},{1,25},{9,1},{17,9},{25,17},{2,26},{10... | collective-permute-start | bytes 393224 | tf_op jit(solution)/shard_map/ppermute | solution.py:41
  7.1 22.3 %collective-permute-start.1 = (bf16[64,1024]{0,1:T(8,128)(2,1)S(1)}, bf16[64,1024]{0,1:T(8,128)(2,1)S(1)}, u32[]{:S(2)}, u32[]{:S(2)}) collective-permute-start(bf16[64,1024]{0,1:T(8,128)(2,1)S(1)} %copy.12), channel_id=1, source_target_pairs={{0,16},{8,24},{16,0},{24,8},{1,17},{9,25},{17,1},{25,9},{2,18},{10... | collective-permute-start | bytes 393224 | tf_op jit(solution)/shard_map/ppermute | solution.py:41
  7.1 22.3 %collective-permute-start = (bf16[64,1024]{0,1:T(8,128)(2,1)S(1)}, bf16[64,1024]{0,1:T(8,128)(2,1)S(1)}, u32[]{:S(2)}, u32[]{:S(2)}) collective-permute-start(bf16[64,1024]{0,1:T(8,128)(2,1)S(1)} %copy.12), channel_id=1, source_target_pairs={{0,8},{8,16},{16,24},{24,0},{1,9},{9,17},{17,25},{25,1},{2,10},{10... | collective-permute-start | bytes 393224 | tf_op jit(solution)/shard_map/ppermute | solution.py:41
  30.4 13.0 %collective-permute-start.3 = (bf16[192,1024]{0,1:T(8,128)(2,1)}, bf16[192,1024]{0,1:T(8,128)(2,1)S(1)}, u32[]{:S(2)}, u32[]{:S(2)}) collective-permute-start(bf16[192,1024]{0,1:T(8,128)(2,1)} %pad_maximum_fusion), channel_id=1, source_target_pairs={{0,1},{1,0},{2,3},{3,2},{4,5},{5,4},{6,7},{7,6},{8,9},{9,8},{10,11... | collective-permute-start | bytes 1179656 | tf_op jit(solution)/shard_map/ppermute | solution.py:31
  32.1 19.2 %collective-permute-start.14 = (bf16[64,1024]{0,1:T(8,128)(2,1)S(1)}, bf16[64,1024]{0,1:T(8,128)(2,1)S(1)}, u32[]{:S(2)}, u32[]{:S(2)}) collective-permute-start(bf16[64,1024]{0,1:T(8,128)(2,1)S(1)} %copy.14), channel_id=1, source_target_pairs={{0,24},{8,0},{16,8},{24,16},{1,25},{9,1},{17,9},{25,17},{2,26},{10... | collective-permute-start | bytes 393224 | tf_op jit(solution)/shard_map/ppermute | solution.py:41
  32.2 25.1 %collective-permute-start.13 = (bf16[64,1024]{0,1:T(8,128)(2,1)S(1)}, bf16[64,1024]{0,1:T(8,128)(2,1)S(1)}, u32[]{:S(2)}, u32[]{:S(2)}) collective-permute-start(bf16[64,1024]{0,1:T(8,128)(2,1)S(1)} %copy.14), channel_id=1, source_target_pairs={{0,16},{8,24},{16,0},{24,8},{1,17},{9,25},{17,1},{25,9},{2,18},{10... | collective-permute-start | bytes 393224 | tf_op jit(solution)/shard_map/ppermute | solution.py:41
  35.1 22.3 %collective-permute-start.12 = (bf16[64,1024]{0,1:T(8,128)(2,1)S(1)}, bf16[64,1024]{0,1:T(8,128)(2,1)S(1)}, u32[]{:S(2)}, u32[]{:S(2)}) collective-permute-start(bf16[64,1024]{0,1:T(8,128)(2,1)S(1)} %copy.14), channel_id=1, source_target_pairs={{0,8},{8,16},{16,24},{24,0},{1,9},{9,17},{17,25},{25,1},{2,10},{10... | collective-permute-start | bytes 393224 | tf_op jit(solution)/shard_map/ppermute | solution.py:41
  51.3 26.5 %collective-permute-start.4 = (bf16[256,1920]{1,0:T(8,128)(2,1)}, bf16[256,1920]{1,0:T(8,128)(2,1)}, u32[]{:S(2)}, u32[]{:S(2)}) collective-permute-start(bf16[256,1920]{1,0:T(8,128)(2,1)} %convolution_convert_fusion.1), channel_id=1, source_target_pairs={{0,2},{2,0},{4,6},{6,4},{1,3},{3,1},{5,7},{7,5},{8,10},{10,8},{12,... | collective-permute-start | bytes 2949128 | tf_op jit(solution)/shard_map/ppermute | solution.py:31
  57.6 12.3 %collective-permute-start.15 = (bf16[192,1024]{0,1:T(8,128)(2,1)S(1)}, bf16[192,1024]{0,1:T(8,128)(2,1)S(1)}, u32[]{:S(2)}, u32[]{:S(2)}) collective-permute-start(bf16[192,1024]{0,1:T(8,128)(2,1)S(1)} %pad_maximum_fusion.1), channel_id=1, source_target_pairs={{0,1},{1,0},{2,3},{3,2},{4,5},{5,4},{6,7},{7,6},{8,9},{9,8},{10,11... | collective-permute-start | bytes 1179656 | tf_op jit(solution)/shard_map/ppermute | solution.py:31
  77.8 5.3 %collective-permute-start.16 = (bf16[256,1920]{1,0:T(8,128)(2,1)}, bf16[256,1920]{1,0:T(8,128)(2,1)}, u32[]{:S(2)}, u32[]{:S(2)}) collective-permute-start(bf16[256,1920]{1,0:T(8,128)(2,1)} %convolution_convert_fusion), channel_id=1, source_target_pairs={{0,2},{2,0},{4,6},{6,4},{1,3},{3,1},{5,7},{7,5},{8,10},{10,8},{12,... | collective-permute-start | bytes 2949128 | tf_op jit(solution)/shard_map/ppermute | solution.py:31
  81.4 24.8 %collective-permute-start.5 = (bf16[256,1920]{1,0:T(8,128)(2,1)S(1)}, bf16[256,1920]{1,0:T(8,128)(2,1)}, u32[]{:S(2)}, u32[]{:S(2)}) collective-permute-start(bf16[256,1920]{1,0:T(8,128)(2,1)S(1)} %fusion), channel_id=1, source_target_pairs={{0,4},{2,6},{4,0},{6,2},{1,5},{3,7},{5,1},{7,3},{8,12},{10,14},{12... | collective-permute-start | bytes 2949128 | tf_op jit(solution)/shard_map/ppermute | solution.py:31
  86.7 40.0 %collective-permute-start.17 = (bf16[256,1920]{1,0:T(8,128)(2,1)S(1)}, bf16[256,1920]{1,0:T(8,128)(2,1)S(1)}, u32[]{:S(2)}, u32[]{:S(2)}) collective-permute-start(bf16[256,1920]{1,0:T(8,128)(2,1)S(1)} %fusion.1), channel_id=1, source_target_pairs={{0,4},{2,6},{4,0},{6,2},{1,5},{3,7},{5,1},{7,3},{8,12},{10,14},{12... | collective-permute-start | bytes 2949128 | tf_op jit(solution)/shard_map/ppermute | solution.py:31
  108.4 30.2 %collective-permute-start.7 = (bf16[256,1920]{1,0:T(8,128)(2,1)S(1)}, bf16[256,1920]{1,0:T(8,128)(2,1)S(1)}, u32[]{:S(2)}, u32[]{:S(2)}) collective-permute-start(bf16[256,1920]{1,0:T(8,128)(2,1)S(1)} %get-tuple-element.6.refs_2_), channel_id=1, source_target_pairs={{0,2},{2,0},{4,6},{6,4},{1,3},{3,1},{5,7},{7,5},{8,10},{10,8},{12,... | collective-permute-start | bytes 2949128 | tf_op jit(solution)/shard_map/ppermute | solution.py:31
  112.0 19.3 %collective-permute-start.6 = (bf16[128,1024]{1,0:T(8,128)(2,1)S(1)}, bf16[128,1024]{1,0:T(8,128)(2,1)S(1)}, u32[]{:S(2)}, u32[]{:S(2)}) collective-permute-start(bf16[128,1024]{1,0:T(8,128)(2,1)S(1)} %bitcast.37), channel_id=1, source_target_pairs={{0,1},{1,0},{2,3},{3,2},{4,5},{5,4},{6,7},{7,6},{8,9},{9,8},{10,11... | collective-permute-start | bytes 786440 | tf_op jit(solution)/shard_map/ppermute | solution.py:31
  130.5 7.9 %collective-permute-start.18 = (bf16[128,1024]{1,0:T(8,128)(2,1)S(1)}, bf16[128,1024]{1,0:T(8,128)(2,1)S(1)}, u32[]{:S(2)}, u32[]{:S(2)}) collective-permute-start(bf16[128,1024]{1,0:T(8,128)(2,1)S(1)} %bitcast.39), channel_id=1, source_target_pairs={{0,1},{1,0},{2,3},{3,2},{4,5},{5,4},{6,7},{7,6},{8,9},{9,8},{10,11... | collective-permute-start | bytes 786440 | tf_op jit(solution)/shard_map/ppermute | solution.py:31
  131.2 11.4 %collective-permute-start.19 = (bf16[256,1920]{1,0:T(8,128)(2,1)S(1)}, bf16[256,1920]{1,0:T(8,128)(2,1)S(1)}, u32[]{:S(2)}, u32[]{:S(2)}) collective-permute-start(bf16[256,1920]{1,0:T(8,128)(2,1)S(1)} %multiply_convert_fusion.refs_2_), channel_id=1, source_target_pairs={{0,2},{2,0},{4,6},{6,4},{1,3},{3,1},{5,7},{7,5},{8,10},{10,8},{12,... | collective-permute-start | bytes 2949128 | tf_op jit(solution)/shard_map/ppermute | solution.py:31
  142.1 15.8 %collective-permute-start.8 = (bf16[128,1024]{1,0:T(8,128)(2,1)S(1)}, bf16[128,1024]{1,0:T(8,128)(2,1)S(1)}, u32[]{:S(2)}, u32[]{:S(2)}) collective-permute-start(bf16[128,1024]{1,0:T(8,128)(2,1)S(1)} %bitcast.38), channel_id=1, source_target_pairs={{0,1},{1,0},{2,3},{3,2},{4,5},{5,4},{6,7},{7,6},{8,9},{9,8},{10,11... | collective-permute-start | bytes 786440 | tf_op jit(solution)/shard_map/ppermute | solution.py:31
  146.1 15.5 %collective-permute-start.20 = (bf16[128,1024]{1,0:T(8,128)(2,1)S(1)}, bf16[128,1024]{1,0:T(8,128)(2,1)S(1)}, u32[]{:S(2)}, u32[]{:S(2)}) collective-permute-start(bf16[128,1024]{1,0:T(8,128)(2,1)S(1)} %bitcast.36), channel_id=1, source_target_pairs={{0,1},{1,0},{2,3},{3,2},{4,5},{5,4},{6,7},{7,6},{8,9},{9,8},{10,11... | collective-permute-start | bytes 786440 | tf_op jit(solution)/shard_map/ppermute | solution.py:31
  158.2 10.5 %collective-permute-start.9 = (bf16[64,1024]{1,0:T(8,128)(2,1)S(1)}, bf16[64,1024]{1,0:T(8,128)(2,1)S(1)}, u32[]{:S(2)}, u32[]{:S(2)}) collective-permute-start(bf16[64,1024]{1,0:T(8,128)(2,1)S(1)} %get-tuple-element.24), channel_id=1, source_target_pairs={{0,24},{8,0},{16,8},{24,16},{1,25},{9,1},{17,9},{25,17},{2,26},{10... | collective-permute-start | bytes 393224 | tf_op jit(solution)/shard_map/ppermute | solution.py:41
  158.2 10.5 %collective-permute-start.11 = (bf16[64,1024]{1,0:T(8,128)(2,1)S(1)}, bf16[64,1024]{1,0:T(8,128)(2,1)S(1)}, u32[]{:S(2)}, u32[]{:S(2)}) collective-permute-start(bf16[64,1024]{1,0:T(8,128)(2,1)S(1)} %get-tuple-element.25), channel_id=1, source_target_pairs={{0,8},{8,16},{16,24},{24,0},{1,9},{9,17},{17,25},{25,1},{2,10},{10... | collective-permute-start | bytes 393224 | tf_op jit(solution)/shard_map/ppermute | solution.py:41
  160.2 17.5 %collective-permute-start.10 = (bf16[64,1024]{1,0:T(8,128)(2,1)S(1)}, bf16[64,1024]{1,0:T(8,128)(2,1)S(1)}, u32[]{:S(2)}, u32[]{:S(2)}) collective-permute-start(bf16[64,1024]{1,0:T(8,128)(2,1)S(1)} %get-tuple-element.26), channel_id=1, source_target_pairs={{0,16},{8,24},{16,0},{24,8},{1,17},{9,25},{17,1},{25,9},{2,18},{10... | collective-permute-start | bytes 393224 | tf_op jit(solution)/shard_map/ppermute | solution.py:41
  161.9 16.6 %collective-permute-start.21 = (bf16[64,1024]{1,0:T(8,128)(2,1)S(1)}, bf16[64,1024]{1,0:T(8,128)(2,1)S(1)}, u32[]{:S(2)}, u32[]{:S(2)}) collective-permute-start(bf16[64,1024]{1,0:T(8,128)(2,1)S(1)} %get-tuple-element.14), channel_id=1, source_target_pairs={{0,24},{8,0},{16,8},{24,16},{1,25},{9,1},{17,9},{25,17},{2,26},{10... | collective-permute-start | bytes 393224 | tf_op jit(solution)/shard_map/ppermute | solution.py:41
  162.9 15.6 %collective-permute-start.23 = (bf16[64,1024]{1,0:T(8,128)(2,1)S(1)}, bf16[64,1024]{1,0:T(8,128)(2,1)S(1)}, u32[]{:S(2)}, u32[]{:S(2)}) collective-permute-start(bf16[64,1024]{1,0:T(8,128)(2,1)S(1)} %get-tuple-element.15), channel_id=1, source_target_pairs={{0,8},{8,16},{16,24},{24,0},{1,9},{9,17},{17,25},{25,1},{2,10},{10... | collective-permute-start | bytes 393224 | tf_op jit(solution)/shard_map/ppermute | solution.py:41
  168.7 13.5 %collective-permute-start.22 = (bf16[64,1024]{1,0:T(8,128)(2,1)S(1)}, bf16[64,1024]{1,0:T(8,128)(2,1)S(1)}, u32[]{:S(2)}, u32[]{:S(2)}) collective-permute-start(bf16[64,1024]{1,0:T(8,128)(2,1)S(1)} %get-tuple-element.16), channel_id=1, source_target_pairs={{0,16},{8,24},{16,0},{24,8},{1,17},{9,25},{17,1},{25,9},{2,18},{10... | collective-permute-start | bytes 393224 | tf_op jit(solution)/shard_map/ppermute | solution.py:41
